TPU v7x, 32 devices: a whole 2x2x4 slice. The times are simulated.
32 devices in a mesh: rep: 4 (over y, core), shard: 8 (over z, x).
Axes of the slice: x: 2, y: 2, z: 4, core: 2. Of those that a mesh axis runs over, the one named last changes fastest.
Arguments:
- tokens: bfloat16 [64, 1024, 512], P('rep', 'shard'), may hold values from -6 to 6
- cotangent: bfloat16 [64, 1024, 512], P('rep', 'shard'), may hold values from -6 to 6
- doc_lengths: int32 [64, 16], P('rep'), may hold values from 1 to 768, 1024 in all within a row
- attend: bfloat16 [512, 1536], P('shard'), may hold values from -0.25 to 0.25
- project: bfloat16 [512, 512], P('shard'), may hold values from -2 to 2
- widen: bfloat16 [512, 2048], P('shard'), may hold values from -0.25 to 0.25
- narrow: bfloat16 [2048, 512], P('shard'), may hold values from -0.125 to 0.125
- hidden_bias: bfloat16 [2048], P('shard'), may hold values from -3 to 3
- final_bias: bfloat16 [512], P('shard'), may hold values from -1.796875 to 1.796875
- gain_first: bfloat16 [512], P('shard'), may hold values from 0.5 to 1.5
- shift_first: bfloat16 [512], P('shard'), may hold values from -1.796875 to 1.796875
- gain_second: bfloat16 [512], P('shard'), may hold values from 0.5 to 1.5
- shift_second: bfloat16 [512], P('shard'), may hold values from -1.796875 to 1.796875
Outputs:
- block_out: float32 [64, 1024, 512], P('rep', 'shard')
- tokens_grad: float32 [64, 1024, 512], P('rep', 'shard')
- attend_grad: float32 [512, 1536], P('shard')
- project_grad: float32 [512, 512], P('shard')
- widen_grad: float32 [512, 2048], P('shard')
- narrow_grad: float32 [2048, 512], P('shard')
- hidden_bias_grad: float32 [2048], P('shard')
- final_bias_grad: float32 [512], P('shard')
- gain_first_grad: float32 [512], P('shard')
- shift_first_grad: float32 [512], P('shard')
- gain_second_grad: float32 [512], P('shard')
- shift_second_grad: float32 [512], P('shard')
Inputs may be any that keep to these rules, and one draw needn't show every extreme that they name: `doc_lengths`: row s lists the lengths of the 16 documents packed in order into sequence s; they fill all 1024 positions, and the longest is 768.
All inputs are finite; a program needn't handle non-finite values.
Results may differ from a plain program's by a relative error of at most 0.017.
Values may be sent and summed in bfloat16 or wider, within the bound.
No kernel may reach another device: no remote copies, remote signals or barrier semaphores. Data moves between devices by JAX's collectives and lax.ppermute only.
A program may use at most 192 MiB of HBM per device.

v0:
```python
import functools

import jax
import jax.numpy as jnp
from jax import lax
from jax.experimental import pallas as pl
from jax.experimental.pallas import tpu as pltpu
from jax.sharding import PartitionSpec as P

HEADS = 8
epsilon = 1e-05
masked = -1e30
F32 = jnp.float32
BF = jnp.bfloat16
MIB = 1 << 20


def dot(a, b):
    return jnp.dot(a, b, preferred_element_type=F32)


def dot_nt(a, b):
    return lax.dot_general(a, b, (((1,), (1,)), ((), ())), preferred_element_type=F32)


def dot_tn(a, b):
    return lax.dot_general(a, b, (((0,), (0,)), ((), ())), preferred_element_type=F32)


def normed(v):
    center = v - jnp.mean(v, axis=-1, keepdims=True)
    rstd = lax.rsqrt(jnp.mean(center * center, axis=-1, keepdims=True) + epsilon)
    return center * rstd, rstd


def norm_back(e, n, rstd):
    return rstd * (
        e - jnp.mean(e, axis=-1, keepdims=True) - n * jnp.mean(e * n, axis=-1, keepdims=True)
    )


def two_heads_lanes(t):
    half = t.shape[0] // 2
    zero = jnp.zeros((half, t.shape[1]), t.dtype)
    left = jnp.concatenate([t[:half], zero], axis=0)
    right = jnp.concatenate([zero, t[half:]], axis=0)
    return jnp.concatenate([left, right], axis=1)


def two_heads_rows(a):
    first = lax.broadcasted_iota(jnp.int32, a.shape, 1) < a.shape[1] // 2
    zero = jnp.zeros_like(a)
    return jnp.concatenate([jnp.where(first, a, zero), jnp.where(first, zero, a)], axis=0)


def diagonal(t):
    rows, cols = t.shape[0] // 2, t.shape[1] // 2
    return jnp.concatenate([t[:rows, :cols], t[rows:, cols:]], axis=0)


def span_bias(doc_from, pooled):
    span = doc_from.shape[1]
    key = lax.broadcasted_iota(jnp.int32, (span, span), 0)
    query = lax.broadcasted_iota(jnp.int32, (span, span), 1)
    direct = jnp.where((key >= doc_from) & (key <= query), 0.0, masked).astype(F32)
    both = jnp.concatenate([direct, pooled], axis=0)
    return jnp.concatenate([both, both], axis=1)


def arriving(meta, sizes, pieces, places, sems, act, kind):
    zs, xs = sizes
    z, x, core = meta[0], meta[1], meta[2]
    at = 0
    for which in range(2):
        half = core if which == 0 else 1 - core
        for kx in range(xs):
            for kz in range(zs):
                shard = (z ^ kz) * xs + (x ^ kx)
                for src, dst in places[kind](pieces, which, kx, kz, shard, half):
                    copy = pltpu.make_async_copy(src, dst, sems.at[kind, at])
                    copy.start() if act == "start" else copy.wait()
                    at += 1


def doc_starts(len_ref, seq):
    starts = [jnp.int32(0)]
    for j in range(len_ref.shape[1] - 1):
        starts.append(starts[-1] + len_ref[seq, j])
    return starts


def start_at(starts, position):
    found = jnp.zeros_like(position)
    for start in starts:
        found = jnp.where(position >= start, start, found)
    return found


def first_member(starts, base, span):
    return jnp.maximum(start_at(starts, base + span - 1) - base, 0)


def prep_kernel(meta, len_ref, x_ref, small_ref, hidden_ref, out_ref, from_ref, pbias_ref, *, sizes, seqs):
    zs, xs = sizes
    z, x = meta[0], meta[1]
    shard = z * xs + x
    nshard, span = pbias_ref.shape[1:]
    width = x_ref.shape[1]
    total = out_ref.shape[0] - small_ref.shape[0] - 4
    step = pl.program_id(0)
    base = shard * span

    @pl.when(step == 0)
    def _():
        def place(v, at):
            row = lax.broadcasted_iota(jnp.int32, (v.shape[1], width), 0)
            lane = lax.broadcasted_iota(jnp.int32, (v.shape[1], width), 1)
            return dot(v, (lane == row + at).astype(F32).astype(BF))

        nsmall, n = small_ref.shape
        rows = [place(small_ref[...], shard * n)]
        for r in range(4):
            rows.append(place(hidden_ref[...], shard * hidden_ref.shape[1] - r * width))
        out_ref[total:, :] = jnp.concatenate(rows, axis=0)

    n, _ = normed(x_ref[...].astype(F32))
    row = lax.broadcasted_iota(jnp.int32, (span, width), 0)
    slot = lax.broadcasted_iota(jnp.int32, (nshard, span), 0)
    slot_span = (z ^ (slot & (zs - 1))) * xs + (x ^ (slot // zs))
    slot_last = slot_span * span + span - 1
    position = base + lax.broadcasted_iota(jnp.int32, (1, span), 1)
    pooled = []
    for i in range(seqs):
        starts = doc_starts(len_ref, step * seqs + i)
        first = first_member(starts, base, span)
        part = jnp.where(row >= first, n[i * span : (i + 1) * span], 0.0)
        count = jnp.full((1, 1), span - first, jnp.int32).astype(F32)
        pooled.append(jnp.sum(part, axis=0, keepdims=True) / count)
        here = start_at(starts, position)
        from_ref[i] = here - base
        last = start_at(starts, slot_last)
        counts = jnp.minimum(span, slot_last + 1 - last).astype(F32)
        seen = (slot_span < shard) & (last == here)
        pbias_ref[i] = jnp.where(seen, jnp.log(counts), masked)
    at = pl.multiple_of(step * seqs, seqs)
    out_ref[pl.ds(at, seqs), :] = jnp.concatenate(pooled, axis=0)


def padded(a, rows, value):
    shape = a.shape[:-2] + (rows - a.shape[-2], a.shape[-1])
    return jnp.concatenate([a, jnp.full(shape, value, a.dtype)], axis=-2) if shape[-2] else a


def vector(slots_ref, i, nslot):
    total = slots_ref.shape[0] // nslot
    at = [k * total + total - 9 + i for k in range(nslot)]
    return sum(slots_ref[k : k + 1, :] for k in at)


def pooled_tokens(slots_ref, seq, nslot, cp):
    total = slots_ref.shape[0] // nslot
    rows = [slots_ref[pl.ds(k * total + seq, 1), :] for k in range(nslot)]
    return padded(jnp.concatenate(rows, axis=0), cp, 0.0)


def attend_kernel(meta, *refs, sizes, seqs, span, rps, start):
    x_ref, slots_ref, from_ref, pbias_ref = refs[:4]
    width = x_ref.shape[1]
    nslot = pbias_ref.shape[1]
    cp = -(-nslot // 16) * 16
    gain, shift = vector(slots_ref, 1, nslot), vector(slots_ref, 2, nslot)
    seq0 = pl.program_id(0) * seqs + start
    if start:
        w_ref, _, _, _, qkv_ref, o_ref, lse_ref = refs[4:]
    else:
        xs = sizes[1]
        pieces = refs[4 : 4 + 2 * xs]
        w_ref, qkv_ref, o_ref, lse_ref, sems = refs[4 + 2 * xs :]
        nh = w_ref.shape[1] // 2

        def place(pieces, which, kx, kz, shard, half):
            yield (
                pieces[which * xs + kx].at[pl.ds(kz * rps, rps), :],
                w_ref.at[
                    pl.ds(pl.multiple_of(shard * rps, rps), rps),
                    pl.ds(pl.multiple_of(half * nh, 128), nh),
                ],
            )

        @pl.when(pl.program_id(0) == 0)
        def _():
            arriving(meta, sizes, pieces, [place], sems, "start", 0)

    n, _ = normed(x_ref[...].astype(F32))
    h = (n * gain + shift).astype(BF)
    pooled_h = jnp.concatenate(
        [pooled_tokens(slots_ref, seq0 + i, nslot, cp) for i in range(seqs)], axis=0
    )
    pooled_h = pooled_h * gain + shift
    if not start:

        @pl.when(pl.program_id(0) == 0)
        def _():
            arriving(meta, sizes, pieces, [place], sems, "wait", 0)

    qkv = dot(h, w_ref[...]).astype(BF)
    q = qkv[:, :width] * jnp.asarray((width // HEADS) ** -0.5, BF)
    qkv_ref[:, :width] = q
    qkv_ref[:, width:] = qkv[:, width:]
    kvb = dot(pooled_h.astype(BF), w_ref[:, width:]).astype(BF)
    pairs = range(HEADS // 2)
    col = lambda part, p: slice(part * width + p * 128, part * width + (p + 1) * 128)
    for s in range(seqs):
        rows = slice(s * span, (s + 1) * span)
        prow = slice(s * cp, (s + 1) * cp)
        bias = span_bias(from_ref[s], padded(pbias_ref[s], cp, masked))
        both = lambda part, p: jnp.concatenate(
            [qkv[rows, col(part, p)], kvb[prow, col(part - 1, p)]], axis=0
        )
        query = [two_heads_lanes(q[rows, col(0, p)].T) for p in pairs]
        scores = [dot(both(1, p), query[p]) + bias for p in pairs]
        top = [jnp.max(scores[p], axis=0, keepdims=True) for p in pairs]
        e = [jnp.exp(scores[p] - top[p]) for p in pairs]
        total = [jnp.sum(e[p], axis=0, keepdims=True) for p in pairs]
        prob = [(e[p] * (1.0 / total[p])).astype(BF) for p in pairs]
        out = [diagonal(dot_tn(both(2, p), prob[p])).astype(BF) for p in pairs]
        for p in pairs:
            lse_ref[s, p : p + 1, :] = top[p] + jnp.log(total[p])
            o_ref[rows, col(0, p)] = out[p].T


def ffn_kernel(meta, *refs, rps, places, nslot):
    o_ref, x_ref, y_ref, slots_ref = refs[:4]
    pieces = refs[4 : 4 + len(places)]
    (
        out_ref,
        dr_ref,
        keep_ref,
        send_ref,
        wp_ref,
        vec_ref,
        all_ref,
        w2_ref,
        acc1_ref,
        acc2_ref,
        accp_ref,
        sems,
    ) = refs[4 + len(places) :]
    hidden, width = w2_ref.shape
    per = hidden // width
    quarter = all_ref.shape[1] // 4
    pq = width // 4
    ph, wh = width // 2, hidden // 2
    step = pl.program_id(0)

    def weights(act):
        z, x, core, pair = meta[0], meta[1], meta[2], meta[3]
        xs = meta[4]
        at = 0
        for ref, place in zip(pieces, places):
            for row, rows, kz, kx, ky, kc, part in place:
                shard = (z ^ kz) * xs + (x ^ kx)
                col = ((pair ^ ky) * 2 + (core ^ kc)) * quarter
                copy = pltpu.make_async_copy(
                    ref.at[pl.ds(row, rows), :],
                    all_ref.at[
                        pl.ds(pl.multiple_of(shard * rps + part, rows), rows),
                        pl.ds(pl.multiple_of(col, 128), quarter),
                    ],
                    sems.at[at],
                )
                copy.start() if act == "start" else copy.wait()
                at += 1

    @pl.when(step == 0)
    def _():
        weights("start")
        acc1_ref[...] = jnp.zeros_like(acc1_ref)
        acc2_ref[...] = jnp.zeros_like(acc2_ref)
        accp_ref[...] = jnp.zeros_like(accp_ref)
        vec_ref[...] = jnp.zeros_like(vec_ref)
        weights("wait")
        for r in range(4):
            wp_ref[:, r * pq : (r + 1) * pq] = all_ref[:, r * quarter : r * quarter + pq]
        at = pq + hidden // 4
        for shard in range(width // rps):
            for b in range(per):
                to = (shard * per + b) * rps
                w2_ref[to : to + rps, :] = all_ref[
                    shard * rps : (shard + 1) * rps, b * quarter + at : b * quarter + at + width
                ]

    o, y = o_ref[...], y_ref[...]
    r1 = x_ref[...].astype(F32) + dot(o, wp_ref[...])
    n, rstd = normed(r1)
    gain = vector(slots_ref, 3, nslot)
    h = (n * gain + vector(slots_ref, 4, nslot)).astype(BF)
    ht = h.T
    out = r1 + vector(slots_ref, 0, nslot)
    dh = jnp.zeros_like(r1)
    for j in range(per):
        at = slice(j * width, (j + 1) * width)
        w1 = all_ref[:, j * quarter + pq : j * quarter + pq + width]
        u = dot(h, w1) + vector(slots_ref, 5 + j, nslot)
        da = dot_nt(y, w2_ref[at, :])
        cdf = 0.5 + 0.5 * lax.erf(u * 0.7071067811865476)
        pdf = jnp.exp(u * u * -0.5) * 0.3989422804014327
        a = (u * cdf).astype(BF)
        du = (da * (cdf + u * pdf)).astype(BF)
        out += dot(a, w2_ref[at, :])
        dh += dot_nt(du, w1)
        acc1_ref[:, at] += dot(ht, du)
        acc2_ref[at, :] += dot_tn(a, y)
        vec_ref[0:1, at] += jnp.sum(du.astype(F32), axis=0, keepdims=True)
    out_ref[...] = out
    yf = y.astype(F32)
    dr = yf + norm_back(dh * gain, n, rstd)
    dr_ref[...] = dr
    accp_ref[...] += dot_tn(o, dr.astype(BF))
    vec_ref[1:2, :width] += jnp.sum(yf, axis=0, keepdims=True)
    vec_ref[2:3, :width] += jnp.sum(dh * n, axis=0, keepdims=True)
    vec_ref[3:4, :width] += jnp.sum(dh, axis=0, keepdims=True)

    @pl.when(step == pl.num_programs(0) - 1)
    def _():
        for which, ref in ((0, keep_ref), (1, send_ref)):
            half = meta[2] if which == 0 else 1 - meta[2]
            pcol = pl.ds(pl.multiple_of(half * ph, 128), ph)
            ref[:, :ph] = accp_ref[:, pcol].astype(BF)
            ref[:, ph : ph + wh] = acc1_ref[:, pl.ds(pl.multiple_of(half * wh, 128), wh)].astype(BF)
            for shard in range(width // rps):
                for j in range(per):
                    at = (shard * per + j) * rps
                    ref[shard * rps : (shard + 1) * rps, ph + wh + j * ph : ph + wh + (j + 1) * ph] = (
                        acc2_ref[at : at + rps, pcol].astype(BF)
                    )


def back_kernel(meta, *refs, seqs, span, begin):
    (
        dr_ref,
        x_ref,
        qkv_ref,
        lse_ref,
        w_ref,
        wp_ref,
        slots_ref,
        from_ref,
        pbias_ref,
    ) = refs[:9]
    if begin:
        dqkv_ref, dpool_ref, acc_ref, dkvb_ref = refs[9:]
    else:
        sum_ref, _, _, dqkv_ref, dpool_ref, keep_ref, send_ref, vec_ref, acc_ref, dkvb_ref = refs[9:]
    width = x_ref.shape[1]
    scale = (width // HEADS) ** -0.5
    step = pl.program_id(0)

    @pl.when(step == 0)
    def _():
        acc_ref[...] = jnp.zeros_like(acc_ref) if begin else sum_ref[...]

    nslot = pbias_ref.shape[1]
    cp = -(-nslot // 16) * 16
    gain, shift = vector(slots_ref, 1, nslot), vector(slots_ref, 2, nslot)
    seq0 = (step + (0 if begin else pl.num_programs(0))) * seqs
    pool = jnp.concatenate(
        [pooled_tokens(slots_ref, seq0 + i, nslot, cp) for i in range(seqs)], axis=0
    )
    pooled_h = (pool * gain + shift).astype(BF)
    kvb = dot(pooled_h, w_ref[:, width:]).astype(BF)
    dr = dr_ref[...]
    do = dot_nt(dr.astype(BF), wp_ref[...]).astype(BF)
    pairs = range(HEADS // 2)
    col = lambda part, p: slice(part * width + p * 128, part * width + (p + 1) * 128)
    for s in range(seqs):
        rows = slice(s * span, (s + 1) * span)
        prow = slice(s * cp, (s + 1) * cp)
        bias = span_bias(from_ref[s], padded(pbias_ref[s], cp, masked))
        both = lambda part, p: jnp.concatenate(
            [qkv_ref[rows, col(part, p)], kvb[prow, col(part - 1, p)]], axis=0
        )
        q = [qkv_ref[rows, col(0, p)] for p in pairs]
        g = [do[rows, col(0, p)] for p in pairs]
        keys = [both(1, p) for p in pairs]
        scores = [dot(keys[p], two_heads_lanes(q[p].T)) + bias for p in pairs]
        dprob = [dot(both(2, p), two_heads_lanes(g[p].T)) for p in pairs]
        prob = [jnp.exp(scores[p] - lse_ref[s, p : p + 1, :]) for p in pairs]
        weighted = [prob[p] * dprob[p] for p in pairs]
        ds = [
            (weighted[p] - prob[p] * jnp.sum(weighted[p], axis=0, keepdims=True)).astype(BF)
            for p in pairs
        ]
        dv = [dot(prob[p].astype(BF), two_heads_rows(g[p])).astype(BF) for p in pairs]
        dq = [(diagonal(dot_tn(keys[p], ds[p])) * scale).astype(BF) for p in pairs]
        dk = [dot(ds[p], two_heads_rows(q[p])).astype(BF) for p in pairs]
        for p in pairs:
            dqkv_ref[rows, col(0, p)] = dq[p].T
            dqkv_ref[rows, col(1, p)] = dk[p][:span]
            dqkv_ref[rows, col(2, p)] = dv[p][:span]
            dkvb_ref[prow, col(0, p)] = dk[p][span:]
            dkvb_ref[prow, col(1, p)] = dv[p][span:]
    n, _ = normed(x_ref[...].astype(F32))
    h = (n * gain + shift).astype(BF)
    dqkv, dkvb = dqkv_ref[...], dkvb_ref[...]
    acc_ref[:width] += dot_tn(h, dqkv)
    acc_ref[:width, width:] += dot_tn(pooled_h, dkvb)
    acc_ref[width : width + 1] += jnp.sum(dqkv.astype(F32), axis=0, keepdims=True)
    acc_ref[width : width + 1, width:] += jnp.sum(dkvb.astype(F32), axis=0, keepdims=True)
    dpool_ref[...] = dot_nt(dkvb, w_ref[:, width:]).astype(BF).reshape(seqs, cp, width)
    if begin:
        return

    @pl.when(step == pl.num_programs(0) - 1)
    def _():
        nh = acc_ref.shape[1] // 2
        for which, ref in ((0, keep_ref), (1, send_ref)):
            half = meta[2] if which == 0 else 1 - meta[2]
            ref[...] = acc_ref[:width, pl.ds(pl.multiple_of(half * nh, 128), nh)].astype(BF)
        w = w_ref[...].astype(F32)

        def row(m):
            total = jnp.sum(m, axis=1, keepdims=True)
            return jnp.broadcast_to(total, (width, 128)).T[:1]

        dshift = row(w * acc_ref[width : width + 1])
        dgain = (row(w * acc_ref[:width]) - shift * dshift) / gain
        vec_ref[0:1] = dgain
        vec_ref[1:2] = dshift


def last_kernel(meta, len_ref, dr_ref, x_ref, dqkv_ref, w_ref, dpool_ref, slots_ref, out_ref, *, seqs, span, nslot):
    n, rstd = normed(x_ref[...].astype(F32))
    dh = dot_nt(dqkv_ref[...], w_ref[...])
    for i in range(seqs):
        starts = doc_starts(len_ref, pl.program_id(0) * seqs + i)
        first = first_member(starts, (meta[0] * meta[4] + meta[1]) * span, span)
        rows = slice(i * span, (i + 1) * span)
        count = jnp.full((1, 1), span - first, jnp.int32).astype(F32)
        share = dpool_ref[i] / count
        row = lax.broadcasted_iota(jnp.int32, (span, n.shape[1]), 0)
        e = (dh[rows] + jnp.where(row >= first, share, 0.0)) * vector(slots_ref, 1, nslot)
        out_ref[rows, :] = dr_ref[rows, :] + norm_back(e, n[rows], rstd[rows])


def after(a, *first):
    return lax.optimization_barrier((a, *first))[0]


def params(mib):
    return pltpu.CompilerParams(dimension_semantics=("arbitrary",), vmem_limit_bytes=mib * MIB)


LITTLE = pl.CostEstimate(flops=1, bytes_accessed=1, transcendentals=0)


def local(
    tokens,
    cotangent,
    doc_lengths,
    attend,
    project,
    widen,
    narrow,
    hidden_bias,
    final_bias,
    gain_first,
    shift_first,
    gain_second,
    shift_second,
    *,
    sizes,
):
    zs, xs, ys, cs = sizes
    nshard = zs * xs
    seq_count, span, width = tokens.shape
    rows = seq_count * span
    hidden = widen.shape[1]
    rps = attend.shape[0]
    rep, shard = lax.axis_index("rep"), lax.axis_index("shard")
    z, x, y, core = shard // xs, shard % xs, rep // cs, rep % cs
    meta = jnp.stack([z, x, core, y % 2, jnp.int32(xs)]).astype(jnp.int32)

    def swap(a, z=0, x=0, y=0, c=0):
        perm = []
        for r in range(ys * cs):
            for s in range(nshard):
                r2 = (r // cs ^ y) * cs + (r % cs ^ c)
                s2 = (s // xs ^ z) * xs + (s % xs ^ x)
                perm.append((r * nshard + s, r2 * nshard + s2))
        return lax.ppermute(a, ("rep", "shard"), perm)

    bits = lambda n: [1 << i for i in range(n.bit_length() - 1)]

    def send(a, dz=0, dx=0, dy=0, dc=0):
        perm = []
        for r in range(ys * cs):
            for s in range(nshard):
                r2 = (r // cs + dy) % ys * cs + (r % cs + dc) % cs
                s2 = (s // xs + dz) % zs * xs + (s % xs + dx) % xs
                perm.append((r * nshard + s, r2 * nshard + s2))
        return lax.ppermute(a, ("rep", "shard"), perm)

    def levels(a):
        return jnp.concatenate([a] + [swap(a, z=k) for k in range(1, zs)], axis=0)

    def sides(a):
        return [a] + [swap(a, x=k) for k in range(1, xs)]

    x2 = tokens.reshape(rows, width)
    y2 = cotangent.reshape(rows, width)
    smem = pl.BlockSpec(memory_space=pltpu.SMEM)
    hbm = pl.BlockSpec(memory_space=pl.ANY)
    nh = attend.shape[1] // 2
    per = hidden // width
    hs = hidden_bias.shape[0]
    attend_col = levels(lax.dynamic_slice_in_dim(attend, core * nh, nh, 1))

    small = jnp.stack([final_bias, gain_first, shift_first, gain_second, shift_second])
    total = seq_count + 5 + 4
    pool_seqs = 8
    packed, doc_from, pbias = pl.pallas_call(
        functools.partial(prep_kernel, sizes=(zs, xs), seqs=pool_seqs),
        grid=(seq_count // pool_seqs,),
        in_specs=[
            smem,
            smem,
            pl.BlockSpec((pool_seqs * span, width), lambda i: (i, 0)),
            pl.BlockSpec((5, rps), lambda i: (0, 0)),
            pl.BlockSpec((1, hs), lambda i: (0, 0)),
        ],
        out_specs=[
            pl.BlockSpec((total, width), lambda i: (0, 0)),
            pl.BlockSpec((pool_seqs, 1, span), lambda i: (i, 0, 0)),
            pl.BlockSpec((pool_seqs, nshard, span), lambda i: (i, 0, 0)),
        ],
        out_shape=[
            jax.ShapeDtypeStruct((total, width), F32),
            jax.ShapeDtypeStruct((seq_count, 1, span), jnp.int32),
            jax.ShapeDtypeStruct((seq_count, nshard, span), F32),
        ],
        compiler_params=params(58),
        cost_estimate=LITTLE,
        name="prep",
    )(meta, doc_lengths, x2, small, hidden_bias[None])
    slots = packed
    for b in bits(zs):
        slots = jnp.concatenate([slots, swap(slots, z=b)], axis=0)
    for b in bits(xs):
        slots = jnp.concatenate([slots, swap(slots, x=b)], axis=0)

    ph, wh = width // 2, hidden // 2
    pair = y % 2
    mine = pair * 2 + core
    cut = lambda a, axis: lax.dynamic_slice_in_dim(
        a, mine * (a.shape[axis] // 4), a.shape[axis] // 4, axis
    )
    ffn_own = jnp.concatenate([cut(project, 1), cut(widen, 1), cut(narrow, 0)], axis=1)
    attend_cols = sides(attend_col)
    attend_parts = attend_cols + [swap(m, c=1) for m in attend_cols]
    ffn_col = levels(after(ffn_own, attend_col)).reshape(zs, rps, -1)
    kr = rps // 2
    over_xs = [ffn_col[:, :kr].reshape(zs * kr, -1)]
    for b in bits(xs):
        over_xs.append(swap(jnp.concatenate(over_xs, axis=0), x=b))
    over_ys = [ffn_col[:, kr:].reshape(zs * kr, -1)]
    over_ys.append(swap(over_ys[0], y=1))

    seqs = 4
    calls = 2
    steps = seq_count // seqs // calls
    all_spec = lambda a, b: pl.BlockSpec((a, b), lambda i, m: (0, 0))
    row_spec = lambda n, w, c=0: pl.BlockSpec((n, w), lambda i, m: (i + c * steps, 0))
    seq_spec = lambda n, a, b, c=0: pl.BlockSpec((n, a, b), lambda i, m: (i + c * steps, 0, 0))
    act_specs = lambda c: [
        row_spec(seqs * span, 3 * width, c),
        row_spec(seqs * span, width, c),
        seq_spec(seqs, HEADS // 2, 2 * span, c),
    ]
    act_shapes = [
        jax.ShapeDtypeStruct((rows, 3 * width), BF),
        jax.ShapeDtypeStruct((rows, width), BF),
        jax.ShapeDtypeStruct((seq_count, HEADS // 2, 2 * span), F32),
    ]

    def attention(c, x2, weights, before):
        return pl.pallas_call(
            functools.partial(
                attend_kernel,
                sizes=(zs, xs),
                seqs=seqs,
                span=span,
                rps=rps,
                start=c * steps * seqs,
            ),
            grid_spec=pltpu.PrefetchScalarGridSpec(
                num_scalar_prefetch=1,
                grid=(steps,),
                in_specs=[
                    row_spec(seqs * span, width, c),
                    all_spec(nshard * total, width),
                    seq_spec(seqs, 1, span, c),
                    seq_spec(seqs, nshard, span, c),
                ]
                + ([all_spec(width, 3 * width)] if c else [hbm] * len(weights))
                + [hbm] * len(before),
                out_specs=([] if c else [all_spec(width, 3 * width)]) + act_specs(c),
                scratch_shapes=[] if c else [pltpu.SemaphoreType.DMA((1, 2 * nshard))],
            ),
            out_shape=([] if c else [jax.ShapeDtypeStruct((width, 3 * width), BF)]) + act_shapes,
            input_output_aliases={6 + i: i for i in range(len(before))},
            compiler_params=params(58),
            cost_estimate=LITTLE,
            name="attention",
        )(meta, x2, slots, doc_from, pbias, *weights, *before)

    w_all, qkv, o, lse = attention(0, after(x2, ffn_col), attend_parts, [])
    over_xs, over_ys = after(over_xs, lse), after(over_ys, lse)
    if len(over_xs) > 1:
        over_xs = [jnp.concatenate(over_xs, axis=0)]
    over_ys = [jnp.concatenate(over_ys, axis=0)]
    both = [over_xs[0], over_ys[0]]
    both_other = [swap(a, c=1) for a in both]
    ends = [swap(over_xs[0], y=1)]
    so_far = over_ys
    for b in bits(xs):
        so_far.append(swap(jnp.concatenate(so_far, axis=0), x=b))
    ends += so_far[1:]
    qkv, o, lse = attention(1, after(x2, *both), [w_all], [qkv, o, lse])
    ends = after(ends, lse)
    ffn_parts = both + both_other + ends + [swap(a, c=1) for a in ends]
    two = [[(kx, 0, 0) for kx in range(xs)], [(0, ky, kr) for ky in range(2)]]
    rest = [[(kx, 1, 0) for kx in range(xs)]]
    rest += [[(kx, ky, kr) for kx in range(b, 2 * b) for ky in range(2)] for b in bits(xs)]
    places = [
        [
            ((i * zs + kz) * kr, kr, kz, kx, ky, kc, part)
            for i, (kx, ky, part) in enumerate(units)
            for kz in range(zs)
        ]
        for group in (two, rest)
        for kc in range(2)
        for units in group
    ]

    tile = 512
    packet = ph + wh + per * ph
    steps, cp = 0, -(-nshard // 16) * 16
    block_out, dr, keep_f, send_f, wp_all, vec_f = pl.pallas_call(
        functools.partial(ffn_kernel, rps=rps, places=places, nslot=nshard),
        grid_spec=pltpu.PrefetchScalarGridSpec(
            num_scalar_prefetch=1,
            grid=(rows // tile,),
            in_specs=[
                row_spec(tile, width),
                row_spec(tile, width),
                row_spec(tile, width),
                all_spec(nshard * total, width),
            ]
            + [hbm] * len(ffn_parts),
            out_specs=[
                row_spec(tile, width),
                row_spec(tile, width),
                all_spec(width, packet),
                all_spec(width, packet),
                all_spec(width, width),
                all_spec(8, hidden),
            ],
            scratch_shapes=[
                pltpu.VMEM((width, width + 2 * hidden), BF),
                pltpu.VMEM((hidden, width), BF),
                pltpu.VMEM((width, hidden), F32),
                pltpu.VMEM((hidden, width), F32),
                pltpu.VMEM((width, width), F32),
                pltpu.SemaphoreType.DMA((sum(len(p) for p in places),)),
            ],
        ),
        out_shape=[
            jax.ShapeDtypeStruct((rows, width), F32),
            jax.ShapeDtypeStruct((rows, width), F32),
            jax.ShapeDtypeStruct((width, packet), BF),
            jax.ShapeDtypeStruct((width, packet), BF),
            jax.ShapeDtypeStruct((width, width), BF),
            jax.ShapeDtypeStruct((8, hidden), F32),
        ],
        compiler_params=params(58),
        cost_estimate=LITTLE,
        name="ffn",
    )(meta, o, x2, y2, slots, *ffn_parts)

    def add(parts, kind):
        total = parts[0].astype(F32)
        for p in parts[1:]:
            total = total + p.astype(F32)
        return total.astype(kind)

    def over_x(a):
        piece = lambda dx: lax.dynamic_slice_in_dim(a, (x + dx) % xs, 1, 1)
        return add([send(piece(dx), dx=dx) if dx else piece(0) for dx in range(xs)], BF)

    def over_y(a):
        n = a.shape[-1] // ys
        piece = lambda dy: lax.dynamic_slice_in_dim(a, (y + dy) % ys * n, n, a.ndim - 1)
        return add([send(piece(dy), dy=dy) if dy else piece(0) for dy in range(ys)], BF)

    def over_z(a):
        k = a.shape[0] // zs
        piece = lambda dz: lax.dynamic_slice_in_dim(a, (z + dz) % zs * k, k, 0)
        parts = [send(piece(dz), dz=dz) if dz else piece(0) for dz in range(zs)]
        return add(parts, BF)

    def over_xy(part):
        n = part.shape[1] // ys
        k = part.shape[0] // nshard
        view = part.reshape(zs, xs, k, ys * n)

        def corner(dx, dy):
            at = (0, (x + dx) % xs, 0, (y + dy) % ys * n)
            return lax.dynamic_slice(view, at, (zs, 1, k, n)).reshape(zs * k, n)

        parts = [
            send(corner(dx, dy), dx=dx, dy=dy) if dx or dy else corner(0, 0)
            for dx in range(xs)
            for dy in range(ys)
        ]
        return add(parts, BF)

    def replicas(part):
        found = {
            (dy, dc): send(part, dy=dy, dc=dc) if dy or dc else part
            for dy in range(ys)
            for dc in range(cs)
        }
        total = []
        for at in range(ys * cs):
            picked = jnp.zeros(part.shape, F32)
            for (dy, dc), piece in found.items():
                mine = ((y - dy + ys) % ys == at % ys) & ((core - dc + cs) % cs == at // ys)
                picked = jnp.where(mine, piece.astype(F32), picked)
            total.append(picked)
        return total

    steps = seq_count // seqs // calls

    def back(c, dr, before):
        nacc = width + 8
        sums = [all_spec(nacc, 3 * width)]
        halves = [all_spec(width, 3 * width // 2)] * 2 + [all_spec(8, width)]
        half_shapes = [
            jax.ShapeDtypeStruct((width, 3 * width // 2), BF),
            jax.ShapeDtypeStruct((width, 3 * width // 2), BF),
            jax.ShapeDtypeStruct((8, width), F32),
        ]
        return pl.pallas_call(
            functools.partial(back_kernel, seqs=seqs, span=span, begin=c == 0),
            grid_spec=pltpu.PrefetchScalarGridSpec(
                num_scalar_prefetch=1,
                grid=(steps,),
                in_specs=[
                    row_spec(seqs * span, width, c),
                    row_spec(seqs * span, width, c),
                    row_spec(seqs * span, 3 * width, c),
                    seq_spec(seqs, HEADS // 2, 2 * span, c),
                    all_spec(width, 3 * width),
                    all_spec(width, width),
                    all_spec(nshard * total, width),
                    seq_spec(seqs, 1, span, c),
                    seq_spec(seqs, nshard, span, c),
                ]
                + ((sums + [hbm, hbm]) if c else []),
                out_specs=[row_spec(seqs * span, 3 * width, c), seq_spec(seqs, cp, width, c)]
                + (halves if c else sums),
                scratch_shapes=([pltpu.VMEM((nacc, 3 * width), F32)] if c else [])
                + [pltpu.VMEM((seqs * cp, 2 * width), BF)],
            ),
            out_shape=[
                jax.ShapeDtypeStruct((rows, 3 * width), BF),
                jax.ShapeDtypeStruct((seq_count, cp, width), BF),
            ]
            + (half_shapes if c else [jax.ShapeDtypeStruct((nacc, 3 * width), F32)]),
            input_output_aliases={11: 0, 12: 1} if c else {},
            compiler_params=params(58),
            cost_estimate=LITTLE,
            name="back",
        )(meta, dr, x2, qkv, lse, w_all, wp_all, slots, doc_from, pbias, *before)

    dqkv, dpool, sums = back(0, dr, [])
    part_f = add([keep_f, after(send(send_f, dc=1), sums)], BF)
    dqkv, dpool, keep_a, send_a, vec_a = back(1, after(dr, part_f), [sums, dqkv, dpool])
    kf = part_f.shape[0] // nshard
    view = part_f.reshape(zs, xs, kf, packet)
    first_f = over_x(view[:, :, : kf // 2])
    second_f = over_y(view[:, :, kf // 2 :])

    dpool, keep_a = after((dpool, keep_a), first_f, second_f)
    part_a = add([keep_a, send(send_a, dc=1)], BF)
    part_f = jnp.concatenate([over_y(first_f), over_x(second_f)], axis=2)
    part_f = part_f.reshape(zs * kf, packet // ys)
    share_a = over_xy(part_a)
    share_f = over_z(part_f)
    grad_f = jnp.concatenate(replicas(share_f), axis=1)
    halves = [grad_f[:, i * packet : (i + 1) * packet] for i in range(2)]
    grad_project = jnp.concatenate([h[:, :ph] for h in halves], axis=1)
    grad_widen = jnp.concatenate([h[:, ph : ph + wh] for h in halves], axis=1)
    grad_narrow = jnp.concatenate(
        [
            jnp.concatenate(
                [h[:, ph + wh + j * ph : ph + wh + (j + 1) * ph] for h in halves], axis=1
            )
            for j in range(per)
        ],
        axis=0,
    )

    vec = jnp.concatenate(
        [vec_f[0].reshape(per, width), vec_f[1:2, :width], vec_a[:2], vec_f[2:4, :width]], axis=0
    ).astype(BF)
    nvec = vec.shape[0]
    dp = jnp.transpose(dpool[:, :nshard], (1, 0, 2)).reshape(xs, zs, seq_count, width)
    dp = jnp.concatenate([dp, jnp.broadcast_to(vec, (xs, zs, nvec, width))], axis=2)
    for b in reversed(bits(xs)):
        dp = add([dp[:b], swap(dp[b:], x=b)], BF)
    dp = dp[0]
    for b in reversed(bits(zs)):
        dp = add([dp[:b], swap(dp[b:], z=b)], BF)
    own = dp[0].astype(F32)
    own_vec = jnp.concatenate(
        [lax.dynamic_slice(own[seq_count:].reshape(nvec * width), (shard * hs,), (hs,))]
        + [
            lax.dynamic_slice(own[seq_count + per + i], (shard * rps,), (rps,))
            for i in range(5)
        ]
    ).astype(BF)
    tokens_grad = pl.pallas_call(
        functools.partial(last_kernel, seqs=seqs, span=span, nslot=nshard),
        grid=(seq_count // seqs,),
        in_specs=[
            smem,
            smem,
            pl.BlockSpec((seqs * span, width), lambda i: (i, 0)),
            pl.BlockSpec((seqs * span, width), lambda i: (i, 0)),
            pl.BlockSpec((seqs * span, 3 * width), lambda i: (i, 0)),
            pl.BlockSpec((width, 3 * width), lambda i: (0, 0)),
            pl.BlockSpec((seqs, 1, width), lambda i: (i, 0, 0)),
            pl.BlockSpec((nshard * total, width), lambda i: (0, 0)),
        ],
        out_specs=pl.BlockSpec((seqs * span, width), lambda i: (i, 0)),
        out_shape=jax.ShapeDtypeStruct((rows, width), F32),
        compiler_params=params(58),
        cost_estimate=LITTLE,
        name="last",
    )(
        meta,
        doc_lengths,
        after(dr, part_a),
        x2,
        dqkv,
        w_all,
        own[:seq_count].reshape(seq_count, 1, width),
        slots,
    )

    share_a = over_z(share_a)
    ncol = share_a.shape[1]
    vrows = -(-own_vec.shape[0] // ncol)
    own_vec = jnp.pad(own_vec, (0, vrows * ncol - own_vec.shape[0])).reshape(vrows, ncol)
    found = replicas(jnp.concatenate([share_a, own_vec], axis=0))
    grad_attend = jnp.concatenate([f[:rps] for f in found], axis=1)
    vec = sum(f[rps:] for f in found).reshape(vrows * ncol)
    vecs = [vec[:hs]] + [vec[hs + i * rps : hs + (i + 1) * rps] for i in range(5)]
    return (
        block_out.reshape(tokens.shape),
        tokens_grad.reshape(tokens.shape),
        grad_attend,
        grad_project,
        grad_widen,
        grad_narrow,
        *vecs,
    )


def solution(mesh):
    first = mesh.devices[0]
    xs = len({d.coords[0] for d in first})
    cs = len({d.core_on_chip for d in mesh.devices[:, 0]})
    sizes = (mesh.shape["shard"] // xs, xs, mesh.shape["rep"] // cs, cs)
    row = P("shard", None)
    vec = P("shard")
    act = P("rep", "shard", None)
    return jax.shard_map(
        functools.partial(local, sizes=sizes),
        mesh=mesh,
        in_specs=(act, act, P("rep", None), row, row, row, row) + (vec,) * 6,
        out_specs=(act, act, row, row, row, row) + (vec,) * 6,
        check_vma=False,
    )
```

profile of v0, /device:TPU:0, one launch (start us, length us, event | category | flops | bytes accessed | tf_op | source)
XLA Modules:
  0.0 214.3 jit_solution(9830973108950714915)
XLA Ops:
  0.7 0.9 copy-done
  1.6 3.1 %collective-permute-start = (bf16[64,768]{1,0:T(8,128)(2,1)S(1)}, bf16[64,768]{1,0:T(8,128)(2,1)S(1)}, u32[]{:S(2)}, u32[]{:S(2)}) collective-permute-start(bf16[64,768]{1,0:T(8,128)(2,1)S(1)} %constant_dynamic-slice_fusion.19), channel_id=1, source_target_pairs={{0,2},{1,3},{2,0},{3,1},{4,6},{5,7},{6,4},{7,5},{8,10},{9,11},{10,... | collective-permute-start | bytes 294920 | tf_op jit(solution)/shard_map/ppermute | solution.py:491
  4.7 2.6 %collective-permute-start.1 = (bf16[64,768]{1,0:T(8,128)(2,1)S(1)}, bf16[64,768]{1,0:T(8,128)(2,1)S(1)}, u32[]{:S(2)}, u32[]{:S(2)}) collective-permute-start(bf16[64,768]{1,0:T(8,128)(2,1)S(1)} %constant_dynamic-slice_fusion.19), channel_id=1, source_target_pairs={{0,4},{1,5},{2,6},{3,7},{4,0},{5,1},{6,2},{7,3},{8,12},{9,13},{10,... | collective-permute-start | bytes 294920 | tf_op jit(solution)/shard_map/ppermute | solution.py:491
  7.3 1.2 broadcast_in_dim.6.hidden_ref
  8.5 0.6 stack.37.meta
  9.1 1.3 stack.43.small_ref
  10.4 4.0 %prep.1 = (f32[25,512]{1,0:T(8,128)}, s32[16,1,128]{2,1,0:T(1,128)}, f32[16,8,128]{2,1,0:T(8,128)}) custom-call(s32[5]{0:T(128)} %stack.37.meta, s32[16,16]{1,0:T(8,128)} %len_ref.3, bf16[2048,512]{1,0:T(8,128)(2,1)} %bitcast.47, bf16[5,64]{1,0:T(8,128)(2,1)} %stack.43.small_ref, bf16[1,256]{1,0:T(2,128)(2,1)} %broadcast_in_dim.6.hidden_ref), custom_call_target="tpu_custom_call" | custom-call | flops 1 | bytes 1 | tf_op jit(solution)/shard_map/prep/pallas_call | solution.py:522
  14.4 0.9 collective-permute-start.7
  15.4 0.7 constant_dynamic-slice_fusion.22
  16.1 0.9 constant_dynamic-slice_fusion.20
  17.0 2.0 collective-permute-done.7
  19.0 0.9 pad_maximum_fusion.9
  19.8 2.5 %collective-permute-start.8 = (f32[50,512]{1,0:T(8,128)S(1)}, f32[50,512]{1,0:T(8,128)S(1)}, u32[]{:S(2)}, u32[]{:S(2)}) collective-permute-start(f32[50,512]{1,0:T(8,128)S(1)} %pad_maximum_fusion.9), channel_id=1, source_target_pairs={{0,4},{1,5},{2,6},{3,7},{4,0},{5,1},{6,2},{7,3},{8,12},{9,13},{10,... | collective-permute-start | bytes 307208 | tf_op jit(solution)/shard_map/ppermute | solution.py:491
  22.3 2.1 collective-permute-start.3
  24.4 2.4 %collective-permute-start.5 = (bf16[64,1152]{1,0:T(8,128)(2,1)S(1)}, bf16[64,1152]{1,0:T(8,128)(2,1)S(1)}, u32[]{:S(2)}, u32[]{:S(2)}) collective-permute-start(bf16[64,1152]{1,0:T(8,128)(2,1)S(1)} %pad_maximum_fusion.7), channel_id=1, source_target_pairs={{0,6},{1,7},{2,4},{3,5},{4,2},{5,3},{6,0},{7,1},{8,14},{9,15},{10,... | collective-permute-start | bytes 442376 | tf_op jit(solution)/shard_map/ppermute | solution.py:491
  26.8 1.5 collective-permute-start.10
  28.3 0.9 collective-permute-done.8
  29.2 2.5 %collective-permute-start.9 = (f32[100,512]{1,0:T(8,128)S(1)}, f32[100,512]{1,0:T(8,128)S(1)}, u32[]{:S(2)}, u32[]{:S(2)}) collective-permute-start(f32[100,512]{1,0:T(8,128)S(1)} %pad_maximum_fusion.6), channel_id=1, source_target_pairs={{0,1},{1,0},{2,3},{3,2},{4,5},{5,4},{6,7},{7,6},{8,9},{9,8},{10,11... | collective-permute-start | bytes 614408 | tf_op jit(solution)/shard_map/ppermute | solution.py:491
  31.7 5.0 %collective-permute-done.4 = bf16[64,1152]{1,0:T(8,128)(2,1)S(1)} collective-permute-done((bf16[64,1152]{1,0:T(8,128)(2,1)S(1)}, bf16[64,1152]{1,0:T(8,128)(2,1)S(1)}, u32[]{:S(2)}, u32[]{:S(2)}) %collective-permute-start.4) | collective-permute-done | bytes 147488 | tf_op jit(solution)/shard_map/ppermute | solution.py:491
  36.9 2.0 collective-permute-start.13
  39.0 1.5 collective-permute-start.6
  40.5 0.8 pad_maximum_fusion.3.refs_1_.refs_3_.refs_6_.slots_ref
  41.3 0.7 copy-done.16
  42.2 10.1 %attention.2 = (bf16[512,1536]{1,0:T(8,128)(2,1)}, bf16[2048,1536]{1,0:T(8,128)(2,1)}, bf16[2048,512]{1,0:T(8,128)(2,1)}, f32[16,4,256]{2,1,0:T(4,128)}) custom-call(s32[5]{0:T(128)} %stack.37.meta, bf16[2048,512]{1,0:T(8,128)(2,1)} %bitcast.48, f32[200,512]{1,0:T(8,128)} %pad_maximum_fusion.3.refs_1_.refs_3_.refs_6_.slots_ref, ...), custom_call_target="tpu_custom_call" | custom-call | flops 1 | bytes 1 | tf_op jit(solution)/shard_map/attention/pallas_call | solution.py:587
  53.1 1.5 collective-permute-start.16
  55.1 9.3 %attention.3 = (bf16[2048,1536]{1,0:T(8,128)(2,1)}, bf16[2048,512]{1,0:T(8,128)(2,1)}, f32[16,4,256]{2,1,0:T(4,128)}) custom-call(s32[5]{0:T(128)} %stack.37.meta, bf16[2048,512]{1,0:T(8,128)(2,1)} %bitcast.49, f32[200,512]{1,0:T(8,128)} %pad_maximum_fusion.3.refs_1_.refs_3_.refs_6_.slots_ref, ...), custom_call_target="tpu_custom_call", output_to_operand_aliasing={{0}: (6, {}), {1}: (7, {}), {2}: (8, {})} | custom-call | flops 1 | bytes 1 | tf_op jit(solution)/shard_map/attention/pallas_call | solution.py:587
  64.4 3.3 %collective-permute-done.17.refs_9_ = bf16[256,1152]{1,0:T(8,128)(2,1)S(1)} collective-permute-done((bf16[256,1152]{1,0:T(8,128)(2,1)S(1)}, bf16[256,1152]{1,0:T(8,128)(2,1)S(1)}, u32[]{:S(2)}, u32[]{:S(2)}) %collective-permute-start.17) | collective-permute-done | bytes 589856 | tf_op jit(solution)/shard_map/ppermute | solution.py:491
  68.6 1.5 collective-permute-done.18.refs_10_
  70.0 0.8 collective-permute-done.19.refs_11_
  70.9 0.8 copy-done.13
  71.7 43.2 %ffn.1 = (f32[2048,512]{1,0:T(8,128)}, f32[2048,512]{1,0:T(8,128)}, bf16[512,2304]{1,0:T(8,128)(2,1)}, bf16[512,2304]{1,0:T(8,128)(2,1)}, bf16[512,512]{1,0:T(8,128)(2,1)}, /*index=5*/f32[8,2048]{1,0:T(8,128)}) custom-call(s32[5]{0:T(128)} %stack.37.meta, bf16[2048,512]{1,0:T(8,128)(2,1)} %get-tuple-element.64.refs_0_, bf16[2048,512]{1,0:T(8,128)(2,1)} %bitcast.50, ...), custom_call_target="tpu_custom_call" | custom-call | flops 1 | bytes 1 | tf_op jit(solution)/shard_map/ffn/pallas_call | solution.py:649
  115.2 14.0 %back.2 = (bf16[2048,1536]{1,0:T(8,128)(2,1)}, bf16[16,16,512]{2,1,0:T(8,128)(2,1)}, f32[520,1536]{1,0:T(8,128)}) custom-call(s32[5]{0:T(128)} %stack.37.meta, f32[2048,512]{1,0:T(8,128)} %get-tuple-element.83.refs_0_.dr_ref, bf16[2048,512]{1,0:T(8,128)(2,1)} %bitcast.51, bf16[2048,1536]{1,0:T(8,128)(2,1)} %get-tuple-element.72.refs_2_, ...), custom_call_target="tpu_custom_call" | custom-call | flops 1 | bytes 1 | tf_op jit(solution)/shard_map/back/pallas_call | solution.py:754
  130.5 0.8 convert.38
  131.4 1.7 collective-permute-start.21
  133.1 15.9 %back.3 = (bf16[2048,1536]{1,0:T(8,128)(2,1)}, bf16[16,16,512]{2,1,0:T(8,128)(2,1)}, bf16[512,768]{1,0:T(8,128)(2,1)}, bf16[512,768]{1,0:T(8,128)(2,1)}, f32[8,512]{1,0:T(8,128)}) custom-call(s32[5]{0:T(128)} %stack.37.meta, f32[2048,512]{1,0:T(8,128)} %get-tuple-element.83.refs_0_.dr_ref, ...), custom_call_target="tpu_custom_call", output_to_operand_aliasing={{0}: (11, {}), {1}: (12, {})} | custom-call | flops 1 | bytes 1 | tf_op jit(solution)/shard_map/back/pallas_call | solution.py:754
  149.0 0.7 slice.295
  150.1 0.6 copy-done.7
  151.5 4.3 %collective-permute-done.24 = bf16[1,4,25,512]{3,1,2,0:T(4,128)(2,1)S(1)} collective-permute-done((bf16[1,4,25,512]{3,1,2,0:T(4,128)(2,1)S(1)}, bf16[1,4,25,512]{3,1,2,0:T(4,128)(2,1)S(1)}, u32[]{:S(2)}, u32[]{:S(2)}) %collective-permute-start.24) | collective-permute-done | bytes 102432 | tf_op jit(solution)/shard_map/ppermute | solution.py:491
  155.9 4.3 %collective-permute-start.25 = (bf16[2,25,512]{2,0,1:T(2,128)(2,1)S(1)}, bf16[2,25,512]{2,0,1:T(2,128)(2,1)S(1)}, u32[]{:S(2)}, u32[]{:S(2)}) collective-permute-start(bf16[2,25,512]{2,0,1:T(2,128)(2,1)S(1)} %slice_bitcast_fusion.1), channel_id=1, source_target_pairs={{0,4},{1,5},{2,6},{3,7},{4,0},{5,1},{6,2},{7,3},{8,12},{9,13},{10,... | collective-permute-start | bytes 153608 | tf_op jit(solution)/shard_map/ppermute | solution.py:491
  160.2 2.4 %collective-permute-done.25 = bf16[2,25,512]{2,0,1:T(2,128)(2,1)S(1)} collective-permute-done((bf16[2,25,512]{2,0,1:T(2,128)(2,1)S(1)}, bf16[2,25,512]{2,0,1:T(2,128)(2,1)S(1)}, u32[]{:S(2)}, u32[]{:S(2)}) %collective-permute-start.25) | collective-permute-done | bytes 51232 | tf_op jit(solution)/shard_map/ppermute | solution.py:491
  162.8 2.1 collective-permute-start.26
  164.9 0.9 collective-permute-start.36
  165.8 1.2 collective-permute-start.37
  167.8 0.6 slice_bitcast_fusion.3.dpool_ref
  168.4 1.3 add_convert_fusion.1
  169.8 1.6 collective-permute-start.27
  171.9 1.4 collective-permute-start.29
  173.4 10.1 %last.1 = f32[2048,512]{1,0:T(8,128)} custom-call(s32[5]{0:T(128)} %stack.37.meta, s32[16,16]{1,0:T(8,128)} %len_ref.3, f32[2048,512]{1,0:T(8,128)} %get-tuple-element.83.refs_0_.dr_ref, bf16[2048,512]{1,0:T(8,128)(2,1)} %bitcast.53, bf16[2048,1536]{1,0:T(8,128)(2,1)} %get-tuple-element.84.dqkv_ref, bf16[512,1536]{1,0:T(8,128)(2,1)} %get-tuple-element.61.refs_4_.w_ref, ...), custom_call_target="tpu_custom_call" | custom-call | flops 1 | bytes 1 | tf_op jit(solution)/shard_map/last/pallas_call | solution.py:834
  184.0 2.1 collective-permute-start.30
  186.0 2.9 %collective-permute-start.31 = (bf16[64,384]{1,0:T(8,128)(2,1)S(1)}, bf16[64,384]{1,0:T(8,128)(2,1)S(1)}, u32[]{:S(2)}, u32[]{:S(2)}) collective-permute-start(bf16[64,384]{1,0:T(8,128)(2,1)S(1)} %get-tuple-element.116), channel_id=1, source_target_pairs={{0,4},{1,5},{2,6},{3,7},{4,0},{5,1},{6,2},{7,3},{8,12},{9,13},{10,... | collective-permute-start | bytes 147464 | tf_op jit(solution)/shard_map/ppermute | solution.py:502
  188.9 0.9 collective-permute-start.32
  189.9 1.2 collective-permute-start.38
  191.2 2.6 %collective-permute-start.40 = (bf16[64,1152]{1,0:T(8,128)(2,1)S(1)}, bf16[64,1152]{1,0:T(8,128)(2,1)S(1)}, u32[]{:S(2)}, u32[]{:S(2)}) collective-permute-start(bf16[64,1152]{1,0:T(8,128)(2,1)S(1)} %get-tuple-element.98), channel_id=1, source_target_pairs={{0,6},{1,7},{2,0},{3,1},{4,2},{5,3},{6,4},{7,5},{8,14},{9,15},{10,... | collective-permute-start | bytes 442376 | tf_op jit(solution)/shard_map/ppermute | solution.py:502
  193.8 1.3 collective-permute-done.31
  195.2 1.3 collective-permute-start.34
  196.5 1.3 collective-permute-done.38
  197.8 4.6 %collective-permute-done.39 = bf16[64,1152]{1,0:T(8,128)(2,1)S(1)} collective-permute-done((bf16[64,1152]{1,0:T(8,128)(2,1)S(1)}, bf16[64,1152]{1,0:T(8,128)(2,1)S(1)}, u32[]{:S(2)}, u32[]{:S(2)}) %collective-permute-start.39) | collective-permute-done | bytes 147488 | tf_op jit(solution)/shard_map/ppermute | solution.py:502
  202.6 1.4 collective-permute-start.42
  205.2 0.8 pad_maximum_fusion.5
  206.6 2.1 collective-permute-done.41
  208.7 2.9 %collective-permute-done.42 = bf16[64,1152]{1,0:T(8,128)(2,1)S(1)} collective-permute-done((bf16[64,1152]{1,0:T(8,128)(2,1)S(1)}, bf16[64,1152]{1,0:T(8,128)(2,1)S(1)}, u32[]{:S(2)}, u32[]{:S(2)}) %collective-permute-start.42) | collective-permute-done | bytes 147488 | tf_op jit(solution)/shard_map/ppermute | solution.py:502
  211.9 0.8 fusion
  212.8 0.7 pad_maximum_fusion.8
  213.4 0.9 maximum_maximum_fusion
  (153 shorter events, 9.7 us)
Async XLA Ops:
  0.6 0.9 copy-start
  1.6 20.7 %collective-permute-start = (bf16[64,768]{1,0:T(8,128)(2,1)S(1)}, bf16[64,768]{1,0:T(8,128)(2,1)S(1)}, u32[]{:S(2)}, u32[]{:S(2)}) collective-permute-start(bf16[64,768]{1,0:T(8,128)(2,1)S(1)} %constant_dynamic-slice_fusion.19), channel_id=1, source_target_pairs={{0,2},{1,3},{2,0},{3,1},{4,6},{5,7},{6,4},{7,5},{8,10},{9,11},{10,... | collective-permute-start | bytes 294920 | tf_op jit(solution)/shard_map/ppermute | solution.py:491
  4.7 17.6 %collective-permute-start.1 = (bf16[64,768]{1,0:T(8,128)(2,1)S(1)}, bf16[64,768]{1,0:T(8,128)(2,1)S(1)}, u32[]{:S(2)}, u32[]{:S(2)}) collective-permute-start(bf16[64,768]{1,0:T(8,128)(2,1)S(1)} %constant_dynamic-slice_fusion.19), channel_id=1, source_target_pairs={{0,4},{1,5},{2,6},{3,7},{4,0},{5,1},{6,2},{7,3},{8,12},{9,13},{10,... | collective-permute-start | bytes 294920 | tf_op jit(solution)/shard_map/ppermute | solution.py:491
  7.3 15.0 %collective-permute-start.2 = (bf16[64,768]{1,0:T(8,128)(2,1)S(1)}, bf16[64,768]{1,0:T(8,128)(2,1)S(1)}, u32[]{:S(2)}, u32[]{:S(2)}) collective-permute-start(bf16[64,768]{1,0:T(8,128)(2,1)S(1)} %constant_dynamic-slice_fusion.19), channel_id=1, source_target_pairs={{0,6},{1,7},{2,4},{3,5},{4,2},{5,3},{6,0},{7,1},{8,14},{9,15},{10,... | collective-permute-start | bytes 294920 | tf_op jit(solution)/shard_map/ppermute | solution.py:491
  14.4 14.8 %copy-start.14 = (f32[25,512]{1,0:T(8,128)S(1)}, f32[25,512]{1,0:T(8,128)}, u32[]{:S(2)}) copy-start(f32[25,512]{1,0:T(8,128)} %get-tuple-element.52) | copy-start | bytes 153604
  14.4 4.5 %collective-permute-start.7 = (f32[25,512]{1,0:T(8,128)}, f32[25,512]{1,0:T(8,128)S(1)}, u32[]{:S(2)}, u32[]{:S(2)}) collective-permute-start(f32[25,512]{1,0:T(8,128)} %get-tuple-element.52), channel_id=1, source_target_pairs={{0,2},{1,3},{2,0},{3,1},{4,6},{5,7},{6,4},{7,5},{8,10},{9,11},{10,... | collective-permute-start | bytes 153608 | tf_op jit(solution)/shard_map/ppermute | solution.py:491
  19.8 9.4 %collective-permute-start.8 = (f32[50,512]{1,0:T(8,128)S(1)}, f32[50,512]{1,0:T(8,128)S(1)}, u32[]{:S(2)}, u32[]{:S(2)}) collective-permute-start(f32[50,512]{1,0:T(8,128)S(1)} %pad_maximum_fusion.9), channel_id=1, source_target_pairs={{0,4},{1,5},{2,6},{3,7},{4,0},{5,1},{6,2},{7,3},{8,12},{9,13},{10,... | collective-permute-start | bytes 307208 | tf_op jit(solution)/shard_map/ppermute | solution.py:491
  22.3 19.0 %copy-start.3 = (bf16[256,768]{1,0:T(8,128)(2,1)}, bf16[256,768]{1,0:T(8,128)(2,1)S(1)}, u32[]{:S(2)}) copy-start(bf16[256,768]{1,0:T(8,128)(2,1)S(1)} %pad_maximum_fusion.4.refs_4_) | copy-start | bytes 1179652
  22.3 6.9 %collective-permute-start.3 = (bf16[64,1152]{1,0:T(8,128)(2,1)S(1)}, bf16[64,1152]{1,0:T(8,128)(2,1)S(1)}, u32[]{:S(2)}, u32[]{:S(2)}) collective-permute-start(bf16[64,1152]{1,0:T(8,128)(2,1)S(1)} %pad_maximum_fusion.7), channel_id=1, source_target_pairs={{0,2},{1,3},{2,0},{3,1},{4,6},{5,7},{6,4},{7,5},{8,10},{9,11},{10,... | collective-permute-start | bytes 442376 | tf_op jit(solution)/shard_map/ppermute | solution.py:491
  24.4 12.3 %collective-permute-start.4 = (bf16[64,1152]{1,0:T(8,128)(2,1)S(1)}, bf16[64,1152]{1,0:T(8,128)(2,1)S(1)}, u32[]{:S(2)}, u32[]{:S(2)}) collective-permute-start(bf16[64,1152]{1,0:T(8,128)(2,1)S(1)} %pad_maximum_fusion.7), channel_id=1, source_target_pairs={{0,4},{1,5},{2,6},{3,7},{4,0},{5,1},{6,2},{7,3},{8,12},{9,13},{10,... | collective-permute-start | bytes 442376 | tf_op jit(solution)/shard_map/ppermute | solution.py:491
  24.4 12.3 %collective-permute-start.5 = (bf16[64,1152]{1,0:T(8,128)(2,1)S(1)}, bf16[64,1152]{1,0:T(8,128)(2,1)S(1)}, u32[]{:S(2)}, u32[]{:S(2)}) collective-permute-start(bf16[64,1152]{1,0:T(8,128)(2,1)S(1)} %pad_maximum_fusion.7), channel_id=1, source_target_pairs={{0,6},{1,7},{2,4},{3,5},{4,2},{5,3},{6,0},{7,1},{8,14},{9,15},{10,... | collective-permute-start | bytes 442376 | tf_op jit(solution)/shard_map/ppermute | solution.py:491
  26.8 9.9 %collective-permute-start.10 = (bf16[256,768]{1,0:T(8,128)(2,1)S(1)}, bf16[256,768]{1,0:T(8,128)(2,1)S(1)}, u32[]{:S(2)}, u32[]{:S(2)}) collective-permute-start(bf16[256,768]{1,0:T(8,128)(2,1)S(1)} %pad_maximum_fusion.4.refs_4_), channel_id=1, source_target_pairs={{0,1},{1,0},{2,3},{3,2},{4,5},{5,4},{6,7},{7,6},{8,9},{9,8},{10,11... | collective-permute-start | bytes 1179656 | tf_op jit(solution)/shard_map/ppermute | solution.py:491
  29.2 12.1 %collective-permute-start.11 = (bf16[256,768]{1,0:T(8,128)(2,1)S(1)}, bf16[256,768]{1,0:T(8,128)(2,1)S(1)}, u32[]{:S(2)}, u32[]{:S(2)}) collective-permute-start(bf16[256,768]{1,0:T(8,128)(2,1)S(1)} %pad_maximum_fusion.4.refs_4_), channel_id=1, source_target_pairs={{0,8},{1,9},{2,10},{3,11},{4,12},{5,13},{6,14},{7,15},{8,0},{9,1},... | collective-permute-start | bytes 1179656 | tf_op jit(solution)/shard_map/ppermute | solution.py:491
  29.2 11.2 %collective-permute-start.9 = (f32[100,512]{1,0:T(8,128)S(1)}, f32[100,512]{1,0:T(8,128)S(1)}, u32[]{:S(2)}, u32[]{:S(2)}) collective-permute-start(f32[100,512]{1,0:T(8,128)S(1)} %pad_maximum_fusion.6), channel_id=1, source_target_pairs={{0,1},{1,0},{2,3},{3,2},{4,5},{5,4},{6,7},{7,6},{8,9},{9,8},{10,11... | collective-permute-start | bytes 614408 | tf_op jit(solution)/shard_map/ppermute | solution.py:491
  36.8 4.5 %copy-start.15 = (bf16[256,768]{1,0:T(8,128)(2,1)}, bf16[256,768]{1,0:T(8,128)(2,1)S(1)}, u32[]{:S(2)}) copy-start(bf16[256,768]{1,0:T(8,128)(2,1)S(1)} %collective-permute-done.10.refs_5_) | copy-start | bytes 1179652
  36.8 4.5 %collective-permute-start.12 = (bf16[256,768]{1,0:T(8,128)(2,1)S(1)}, bf16[256,768]{1,0:T(8,128)(2,1)S(1)}, u32[]{:S(2)}, u32[]{:S(2)}) collective-permute-start(bf16[256,768]{1,0:T(8,128)(2,1)S(1)} %collective-permute-done.10.refs_5_), channel_id=1, source_target_pairs={{0,8},{1,9},{2,10},{3,11},{4,12},{5,13},{6,14},{7,15},{8,0},{9,1},... | collective-permute-start | bytes 1179656 | tf_op jit(solution)/shard_map/ppermute | solution.py:491
  36.9 15.4 %collective-permute-start.13 = (bf16[128,1152]{1,0:T(8,128)(2,1)S(1)}, bf16[128,1152]{1,0:T(8,128)(2,1)S(1)}, u32[]{:S(2)}, u32[]{:S(2)}) collective-permute-start(bf16[128,1152]{1,0:T(8,128)(2,1)S(1)} %bitcast.63), channel_id=1, source_target_pairs={{0,16},{1,17},{2,18},{3,19},{4,20},{5,21},{6,22},{7,23},{8,24},{9,... | collective-permute-start | bytes 884744 | tf_op jit(solution)/shard_map/ppermute | solution.py:491
  39.0 13.4 %collective-permute-start.6 = (bf16[128,1152]{1,0:T(8,128)(2,1)S(1)}, bf16[128,1152]{1,0:T(8,128)(2,1)S(1)}, u32[]{:S(2)}, u32[]{:S(2)}) collective-permute-start(bf16[128,1152]{1,0:T(8,128)(2,1)S(1)} %bitcast.61), channel_id=1, source_target_pairs={{0,1},{1,0},{2,3},{3,2},{4,5},{5,4},{6,7},{7,6},{8,9},{9,8},{10,11... | collective-permute-start | bytes 884744 | tf_op jit(solution)/shard_map/ppermute | solution.py:491
  41.3 0.7 copy-start.16
  41.3 0.9 copy-start.17
  52.4 11.9 %copy-start.5 = (bf16[256,1152]{1,0:T(8,128)(2,1)}, bf16[256,1152]{1,0:T(8,128)(2,1)S(1)}, u32[]{:S(2)}) copy-start(bf16[256,1152]{1,0:T(8,128)(2,1)S(1)} %constant_dynamic-update-slice_fusion.2.refs_5_) | copy-start | bytes 1769476
  52.4 15.2 %collective-permute-start.17 = (bf16[256,1152]{1,0:T(8,128)(2,1)S(1)}, bf16[256,1152]{1,0:T(8,128)(2,1)S(1)}, u32[]{:S(2)}, u32[]{:S(2)}) collective-permute-start(bf16[256,1152]{1,0:T(8,128)(2,1)S(1)} %constant_dynamic-update-slice_fusion.2.refs_5_), channel_id=1, source_target_pairs={{0,1},{1,0},{2,3},{3,2},{4,5},{5,4},{6,7},{7,6},{8,9},{9,8},{10,11... | collective-permute-start | bytes 1769480 | tf_op jit(solution)/shard_map/ppermute | solution.py:491
  53.1 11.3 %copy-start.4 = (bf16[256,1152]{1,0:T(8,128)(2,1)}, bf16[256,1152]{1,0:T(8,128)(2,1)S(1)}, u32[]{:S(2)}) copy-start(bf16[256,1152]{1,0:T(8,128)(2,1)S(1)} %constant_dynamic-update-slice_fusion.refs_4_) | copy-start | bytes 1769476
  53.1 15.0 %collective-permute-start.16 = (bf16[256,1152]{1,0:T(8,128)(2,1)S(1)}, bf16[256,1152]{1,0:T(8,128)(2,1)S(1)}, u32[]{:S(2)}, u32[]{:S(2)}) collective-permute-start(bf16[256,1152]{1,0:T(8,128)(2,1)S(1)} %constant_dynamic-update-slice_fusion.refs_4_), channel_id=1, source_target_pairs={{0,16},{1,17},{2,18},{3,19},{4,20},{5,21},{6,22},{7,23},{8,24},{9,... | collective-permute-start | bytes 1769480 | tf_op jit(solution)/shard_map/ppermute | solution.py:491
  54.6 14.0 %collective-permute-start.15 = (bf16[256,1152]{1,0:T(8,128)(2,1)S(1)}, bf16[256,1152]{1,0:T(8,128)(2,1)S(1)}, u32[]{:S(2)}, u32[]{:S(2)}) collective-permute-start(bf16[256,1152]{1,0:T(8,128)(2,1)S(1)} %constant_dynamic-update-slice_fusion.2.refs_5_), channel_id=1, source_target_pairs={{0,8},{1,9},{2,10},{3,11},{4,12},{5,13},{6,14},{7,15},{8,0},{9,1},... | collective-permute-start | bytes 1769480 | tf_op jit(solution)/shard_map/ppermute | solution.py:491
  54.6 14.0 %collective-permute-start.14 = (bf16[256,1152]{1,0:T(8,128)(2,1)S(1)}, bf16[256,1152]{1,0:T(8,128)(2,1)S(1)}, u32[]{:S(2)}, u32[]{:S(2)}) collective-permute-start(bf16[256,1152]{1,0:T(8,128)(2,1)S(1)} %constant_dynamic-update-slice_fusion.refs_4_), channel_id=1, source_target_pairs={{0,8},{1,9},{2,10},{3,11},{4,12},{5,13},{6,14},{7,15},{8,0},{9,1},... | collective-permute-start | bytes 1769480 | tf_op jit(solution)/shard_map/ppermute | solution.py:491
  67.7 3.2 %copy-start.8 = (bf16[256,1152]{1,0:T(8,128)(2,1)}, bf16[256,1152]{1,0:T(8,128)(2,1)S(1)}, u32[]{:S(2)}) copy-start(bf16[256,1152]{1,0:T(8,128)(2,1)S(1)} %collective-permute-done.17.refs_9_) | copy-start | bytes 1769476
  68.0 2.9 %copy-start.9 = (bf16[256,1152]{1,0:T(8,128)(2,1)}, bf16[256,1152]{1,0:T(8,128)(2,1)S(1)}, u32[]{:S(2)}) copy-start(bf16[256,1152]{1,0:T(8,128)(2,1)S(1)} %collective-permute-done.16.refs_8_) | copy-start | bytes 1769476
  68.0 2.0 collective-permute-start.18
  68.0 2.8 %collective-permute-start.19 = (bf16[256,1152]{1,0:T(8,128)(2,1)S(1)}, bf16[256,1152]{1,0:T(8,128)(2,1)S(1)}, u32[]{:S(2)}, u32[]{:S(2)}) collective-permute-start(bf16[256,1152]{1,0:T(8,128)(2,1)S(1)} %collective-permute-done.17.refs_9_), channel_id=1, source_target_pairs={{0,8},{1,9},{2,10},{3,11},{4,12},{5,13},{6,14},{7,15},{8,0},{9,1},... | collective-permute-start | bytes 1769480 | tf_op jit(solution)/shard_map/ppermute | solution.py:491
  68.6 2.3 %copy-start.10 = (bf16[256,1152]{1,0:T(8,128)(2,1)}, bf16[256,1152]{1,0:T(8,128)(2,1)S(1)}, u32[]{:S(2)}) copy-start(bf16[256,1152]{1,0:T(8,128)(2,1)S(1)} %collective-permute-done.15.refs_7_) | copy-start | bytes 1769476
  68.6 2.3 %copy-start.11 = (bf16[256,1152]{1,0:T(8,128)(2,1)}, bf16[256,1152]{1,0:T(8,128)(2,1)S(1)}, u32[]{:S(2)}) copy-start(bf16[256,1152]{1,0:T(8,128)(2,1)S(1)} %collective-permute-done.14.refs_6_) | copy-start | bytes 1769476
  70.0 0.9 copy-start.12
  70.9 0.9 copy-start.13
  115.0 14.2 %collective-permute-start.20 = (bf16[512,2304]{1,0:T(8,128)(2,1)}, bf16[512,2304]{1,0:T(8,128)(2,1)S(1)}, u32[]{:S(2)}, u32[]{:S(2)}) collective-permute-start(bf16[512,2304]{1,0:T(8,128)(2,1)} %get-tuple-element.71), channel_id=1, source_target_pairs={{0,8},{1,9},{2,10},{3,11},{4,12},{5,13},{6,14},{7,15},{8,0},{9,1},... | collective-permute-start | bytes 7077896 | tf_op jit(solution)/shard_map/ppermute | solution.py:502
  115.2 14.0 %copy-start.2 = (bf16[512,2304]{1,0:T(8,128)(2,1)S(1)}, bf16[512,2304]{1,0:T(8,128)(2,1)}, u32[]{:S(2)}) copy-start(bf16[512,2304]{1,0:T(8,128)(2,1)} %get-tuple-element.70) | copy-start | bytes 7077892
  130.0 19.8 %collective-permute-start.22 = (bf16[4,2,32,1152]{3,2,1,0:T(8,128)(2,1)S(1)}, bf16[4,2,32,1152]{3,2,1,0:T(8,128)(2,1)S(1)}, u32[]{:S(2)}, u32[]{:S(2)}) collective-permute-start(bf16[4,2,32,1152]{3,2,1,0:T(8,128)(2,1)S(1)} %constant_dynamic-slice_fusion.17), channel_id=1, source_target_pairs={{0,16},{1,17},{2,18},{3,19},{4,20},{5,21},{6,22},{7,23},{8,24},{9,... | collective-permute-start | bytes 1769480 | tf_op jit(solution)/shard_map/ppermute | solution.py:502
  131.4 18.5 %collective-permute-start.21 = (bf16[4,1,32,2304]{3,2,1,0:T(8,128)(2,1)S(1)}, bf16[4,1,32,2304]{3,2,1,0:T(8,128)(2,1)S(1)}, u32[]{:S(2)}, u32[]{:S(2)}) collective-permute-start(bf16[4,1,32,2304]{3,2,1,0:T(8,128)(2,1)S(1)} %constant_dynamic-slice_fusion.18), channel_id=1, source_target_pairs={{0,1},{1,0},{2,3},{3,2},{4,5},{5,4},{6,7},{7,6},{8,9},{9,8},{10,11... | collective-permute-start | bytes 1769480 | tf_op jit(solution)/shard_map/ppermute | solution.py:502
  149.8 1.0 copy-start.7
  150.8 17.6 %copy-start.6 = (bf16[512,768]{1,0:T(8,128)(2,1)S(1)}, bf16[512,768]{1,0:T(8,128)(2,1)}, u32[]{:S(2)}) copy-start(bf16[512,768]{1,0:T(8,128)(2,1)} %get-tuple-element.81) | copy-start | bytes 2359300
  151.0 4.7 %collective-permute-start.24 = (bf16[1,4,25,512]{3,1,2,0:T(4,128)(2,1)S(1)}, bf16[1,4,25,512]{3,1,2,0:T(4,128)(2,1)S(1)}, u32[]{:S(2)}, u32[]{:S(2)}) collective-permute-start(bf16[1,4,25,512]{3,1,2,0:T(4,128)(2,1)S(1)} %pad_maximum_fusion.10), channel_id=1, source_target_pairs={{0,1},{1,0},{2,3},{3,2},{4,5},{5,4},{6,7},{7,6},{8,9},{9,8},{10,11... | collective-permute-start | bytes 307208 | tf_op jit(solution)/shard_map/ppermute | solution.py:491
  151.5 16.9 %collective-permute-start.23 = (bf16[512,768]{1,0:T(8,128)(2,1)}, bf16[512,768]{1,0:T(8,128)(2,1)}, u32[]{:S(2)}, u32[]{:S(2)}) collective-permute-start(bf16[512,768]{1,0:T(8,128)(2,1)} %get-tuple-element.82), channel_id=1, source_target_pairs={{0,8},{1,9},{2,10},{3,11},{4,12},{5,13},{6,14},{7,15},{8,0},{9,1},... | collective-permute-start | bytes 2359304 | tf_op jit(solution)/shard_map/ppermute | solution.py:502
  155.9 6.8 %collective-permute-start.25 = (bf16[2,25,512]{2,0,1:T(2,128)(2,1)S(1)}, bf16[2,25,512]{2,0,1:T(2,128)(2,1)S(1)}, u32[]{:S(2)}, u32[]{:S(2)}) collective-permute-start(bf16[2,25,512]{2,0,1:T(2,128)(2,1)S(1)} %slice_bitcast_fusion.1), channel_id=1, source_target_pairs={{0,4},{1,5},{2,6},{3,7},{4,0},{5,1},{6,2},{7,3},{8,12},{9,13},{10,... | collective-permute-start | bytes 153608 | tf_op jit(solution)/shard_map/ppermute | solution.py:491
  162.8 4.2 %collective-permute-start.26 = (bf16[1,25,512]{2,0,1:T(2,128)(2,1)S(1)}, bf16[1,25,512]{2,0,1:T(2,128)(2,1)S(1)}, u32[]{:S(2)}, u32[]{:S(2)}) collective-permute-start(bf16[1,25,512]{2,0,1:T(2,128)(2,1)S(1)} %slice.237), channel_id=1, source_target_pairs={{0,2},{1,3},{2,0},{3,1},{4,6},{5,7},{6,4},{7,5},{8,10},{9,11},{10,... | collective-permute-start | bytes 76808 | tf_op jit(solution)/shard_map/ppermute | solution.py:491
  164.9 18.6 %collective-permute-start.36 = (bf16[4,1,32,1152]{3,2,1,0:T(8,128)(2,1)S(1)}, bf16[4,1,32,1152]{3,2,1,0:T(8,128)(2,1)S(1)}, u32[]{:S(2)}, u32[]{:S(2)}) collective-permute-start(bf16[4,1,32,1152]{3,2,1,0:T(8,128)(2,1)S(1)} %constant_dynamic-slice_fusion.4), channel_id=1, source_target_pairs={{0,16},{1,17},{2,18},{3,19},{4,20},{5,21},{6,22},{7,23},{8,24},{9,... | collective-permute-start | bytes 884744 | tf_op jit(solution)/shard_map/ppermute | solution.py:502
  165.8 17.8 %collective-permute-start.37 = (bf16[4,1,32,1152]{3,2,1,0:T(8,128)(2,1)S(1)}, bf16[4,1,32,1152]{3,2,1,0:T(8,128)(2,1)S(1)}, u32[]{:S(2)}, u32[]{:S(2)}) collective-permute-start(bf16[4,1,32,1152]{3,2,1,0:T(8,128)(2,1)S(1)} %constant_dynamic-slice_fusion.3), channel_id=1, source_target_pairs={{0,1},{1,0},{2,3},{3,2},{4,5},{5,4},{6,7},{7,6},{8,9},{9,8},{10,11... | collective-permute-start | bytes 884744 | tf_op jit(solution)/shard_map/ppermute | solution.py:502
  169.8 13.9 %collective-permute-start.27 = (bf16[256,384]{1,0:T(8,128)(2,1)S(1)}, bf16[256,384]{1,0:T(8,128)(2,1)S(1)}, u32[]{:S(2)}, u32[]{:S(2)}) collective-permute-start(bf16[256,384]{1,0:T(8,128)(2,1)S(1)} %bitcast.68), channel_id=1, source_target_pairs={{0,16},{1,17},{2,18},{3,19},{4,20},{5,21},{6,22},{7,23},{8,24},{9,... | collective-permute-start | bytes 589832 | tf_op jit(solution)/shard_map/ppermute | solution.py:502
  171.4 12.4 %collective-permute-start.28 = (bf16[256,384]{1,0:T(8,128)(2,1)S(1)}, bf16[256,384]{1,0:T(8,128)(2,1)S(1)}, u32[]{:S(2)}, u32[]{:S(2)}) collective-permute-start(bf16[256,384]{1,0:T(8,128)(2,1)S(1)} %bitcast.67), channel_id=1, source_target_pairs={{0,1},{1,0},{2,3},{3,2},{4,5},{5,4},{6,7},{7,6},{8,9},{9,8},{10,11... | collective-permute-start | bytes 589832 | tf_op jit(solution)/shard_map/ppermute | solution.py:502
  171.9 11.8 %collective-permute-start.29 = (bf16[256,384]{1,0:T(8,128)(2,1)S(1)}, bf16[256,384]{1,0:T(8,128)(2,1)S(1)}, u32[]{:S(2)}, u32[]{:S(2)}) collective-permute-start(bf16[256,384]{1,0:T(8,128)(2,1)S(1)} %bitcast.66), channel_id=1, source_target_pairs={{0,17},{1,16},{2,19},{3,18},{4,21},{5,20},{6,23},{7,22},{8,25},{9,... | collective-permute-start | bytes 589832 | tf_op jit(solution)/shard_map/ppermute | solution.py:502
  184.0 7.2 %collective-permute-start.30 = (bf16[64,384]{1,0:T(8,128)(2,1)S(1)}, bf16[64,384]{1,0:T(8,128)(2,1)S(1)}, u32[]{:S(2)}, u32[]{:S(2)}) collective-permute-start(bf16[64,384]{1,0:T(8,128)(2,1)S(1)} %get-tuple-element.114), channel_id=1, source_target_pairs={{0,2},{1,3},{2,4},{3,5},{4,6},{5,7},{6,0},{7,1},{8,10},{9,11},{10,... | collective-permute-start | bytes 147464 | tf_op jit(solution)/shard_map/ppermute | solution.py:502
  186.0 9.1 %collective-permute-start.31 = (bf16[64,384]{1,0:T(8,128)(2,1)S(1)}, bf16[64,384]{1,0:T(8,128)(2,1)S(1)}, u32[]{:S(2)}, u32[]{:S(2)}) collective-permute-start(bf16[64,384]{1,0:T(8,128)(2,1)S(1)} %get-tuple-element.116), channel_id=1, source_target_pairs={{0,4},{1,5},{2,6},{3,7},{4,0},{5,1},{6,2},{7,3},{8,12},{9,13},{10,... | collective-permute-start | bytes 147464 | tf_op jit(solution)/shard_map/ppermute | solution.py:502
  188.9 6.2 %collective-permute-start.32 = (bf16[64,384]{1,0:T(8,128)(2,1)S(1)}, bf16[64,384]{1,0:T(8,128)(2,1)S(1)}, u32[]{:S(2)}, u32[]{:S(2)}) collective-permute-start(bf16[64,384]{1,0:T(8,128)(2,1)S(1)} %get-tuple-element.115), channel_id=1, source_target_pairs={{0,6},{1,7},{2,0},{3,1},{4,2},{5,3},{6,4},{7,5},{8,14},{9,15},{10,... | collective-permute-start | bytes 147464 | tf_op jit(solution)/shard_map/ppermute | solution.py:502
  189.9 7.9 %collective-permute-start.38 = (bf16[64,1152]{1,0:T(8,128)(2,1)S(1)}, bf16[64,1152]{1,0:T(8,128)(2,1)S(1)}, u32[]{:S(2)}, u32[]{:S(2)}) collective-permute-start(bf16[64,1152]{1,0:T(8,128)(2,1)S(1)} %get-tuple-element.97), channel_id=1, source_target_pairs={{0,2},{1,3},{2,4},{3,5},{4,6},{5,7},{6,0},{7,1},{8,10},{9,11},{10,... | collective-permute-start | bytes 442376 | tf_op jit(solution)/shard_map/ppermute | solution.py:502
  191.1 11.3 %collective-permute-start.39 = (bf16[64,1152]{1,0:T(8,128)(2,1)S(1)}, bf16[64,1152]{1,0:T(8,128)(2,1)S(1)}, u32[]{:S(2)}, u32[]{:S(2)}) collective-permute-start(bf16[64,1152]{1,0:T(8,128)(2,1)S(1)} %get-tuple-element.99), channel_id=1, source_target_pairs={{0,4},{1,5},{2,6},{3,7},{4,0},{5,1},{6,2},{7,3},{8,12},{9,13},{10,... | collective-permute-start | bytes 442376 | tf_op jit(solution)/shard_map/ppermute | solution.py:502
  191.2 11.2 %collective-permute-start.40 = (bf16[64,1152]{1,0:T(8,128)(2,1)S(1)}, bf16[64,1152]{1,0:T(8,128)(2,1)S(1)}, u32[]{:S(2)}, u32[]{:S(2)}) collective-permute-start(bf16[64,1152]{1,0:T(8,128)(2,1)S(1)} %get-tuple-element.98), channel_id=1, source_target_pairs={{0,6},{1,7},{2,0},{3,1},{4,2},{5,3},{6,4},{7,5},{8,14},{9,15},{10,... | collective-permute-start | bytes 442376 | tf_op jit(solution)/shard_map/ppermute | solution.py:502
  195.2 8.8 %collective-permute-start.33 = (bf16[66,384]{1,0:T(8,128)(2,1)S(1)}, bf16[66,384]{1,0:T(8,128)(2,1)S(1)}, u32[]{:S(2)}, u32[]{:S(2)}) collective-permute-start(bf16[66,384]{1,0:T(8,128)(2,1)S(1)} %pad_maximum_fusion.11), channel_id=1, source_target_pairs={{0,24},{1,25},{2,26},{3,27},{4,28},{5,29},{6,30},{7,31},{8,16},{9,... | collective-permute-start | bytes 152072 | tf_op jit(solution)/shard_map/ppermute | solution.py:502
  195.2 9.2 %collective-permute-start.34 = (bf16[66,384]{1,0:T(8,128)(2,1)S(1)}, bf16[66,384]{1,0:T(8,128)(2,1)S(1)}, u32[]{:S(2)}, u32[]{:S(2)}) collective-permute-start(bf16[66,384]{1,0:T(8,128)(2,1)S(1)} %pad_maximum_fusion.11), channel_id=1, source_target_pairs={{0,16},{1,17},{2,18},{3,19},{4,20},{5,21},{6,22},{7,23},{8,24},{9,... | collective-permute-start | bytes 152072 | tf_op jit(solution)/shard_map/ppermute | solution.py:502
  197.8 6.6 %collective-permute-start.35 = (bf16[66,384]{1,0:T(8,128)(2,1)S(1)}, bf16[66,384]{1,0:T(8,128)(2,1)S(1)}, u32[]{:S(2)}, u32[]{:S(2)}) collective-permute-start(bf16[66,384]{1,0:T(8,128)(2,1)S(1)} %pad_maximum_fusion.11), channel_id=1, source_target_pairs={{0,8},{1,9},{2,10},{3,11},{4,12},{5,13},{6,14},{7,15},{8,0},{9,1},... | collective-permute-start | bytes 152072 | tf_op jit(solution)/shard_map/ppermute | solution.py:502
  202.5 6.2 %collective-permute-start.41 = (bf16[64,1152]{1,0:T(8,128)(2,1)S(1)}, bf16[64,1152]{1,0:T(8,128)(2,1)S(1)}, u32[]{:S(2)}, u32[]{:S(2)}) collective-permute-start(bf16[64,1152]{1,0:T(8,128)(2,1)S(1)} %add_convert_fusion.6), channel_id=1, source_target_pairs={{0,24},{1,25},{2,26},{3,27},{4,28},{5,29},{6,30},{7,31},{8,16},{9,... | collective-permute-start | bytes 442376 | tf_op jit(solution)/shard_map/ppermute | solution.py:502
  202.6 9.0 %collective-permute-start.42 = (bf16[64,1152]{1,0:T(8,128)(2,1)S(1)}, bf16[64,1152]{1,0:T(8,128)(2,1)S(1)}, u32[]{:S(2)}, u32[]{:S(2)}) collective-permute-start(bf16[64,1152]{1,0:T(8,128)(2,1)S(1)} %add_convert_fusion.6), channel_id=1, source_target_pairs={{0,16},{1,17},{2,18},{3,19},{4,20},{5,21},{6,22},{7,23},{8,24},{9,... | collective-permute-start | bytes 442376 | tf_op jit(solution)/shard_map/ppermute | solution.py:502
  204.0 7.7 %collective-permute-start.43 = (bf16[64,1152]{1,0:T(8,128)(2,1)S(1)}, bf16[64,1152]{1,0:T(8,128)(2,1)S(1)}, u32[]{:S(2)}, u32[]{:S(2)}) collective-permute-start(bf16[64,1152]{1,0:T(8,128)(2,1)S(1)} %add_convert_fusion.6), channel_id=1, source_target_pairs={{0,8},{1,9},{2,10},{3,11},{4,12},{5,13},{6,14},{7,15},{8,0},{9,1},... | collective-permute-start | bytes 442376 | tf_op jit(solution)/shard_map/ppermute | solution.py:502
  211.9 2.4 %copy-start.1 = (bf16[64,1536]{1,0:T(8,128)(2,1)S(1)}, bf16[64,1536]{1,0:T(8,128)(2,1)}, u32[]{:S(2)}) copy-start(bf16[64,1536]{1,0:T(8,128)(2,1)} %param.16) | copy-start | bytes 589828
where the time goes:
time: 215 us; the launch traced here: 214 us
  Pallas kernels  107 us (50%)
  starting transfers between devices  52.1 us (24%)
  waiting for transfers between devices  32.9 us (15%)
  local copies, waits for them, and re-layouts  12.3 us (6%)
  other arithmetic  9 us (4%)
    pallas_call x1, Pallas kernels, local(): pl.pallas_call(functools.partial(ffn_kernel, rps=rps, places=places, nslo...  43.2 us
    ppermute x23, starting transfers between devices, swap(): return lax.ppermute(a, ('rep', 'shard'), perm)  31.2 us
    pallas_call x2, Pallas kernels, back(): pl.pallas_call(functools.partial(back_kernel, seqs=seqs, span=span, begin...  29.9 us
    ppermute x21, starting transfers between devices, send(): return lax.ppermute(a, ('rep', 'shard'), perm)  20.9 us
    ppermute x23, waiting for transfers between devices, swap(): return lax.ppermute(a, ('rep', 'shard'), perm)  20.5 us
    pallas_call x2, Pallas kernels, attention(): pl.pallas_call(functools.partial(attend_kernel, sizes=(zs, xs), seqs=seqs...  19.4 us
    ppermute x21, waiting for transfers between devices, send(): return lax.ppermute(a, ('rep', 'shard'), perm)  12.4 us
    pallas_call x1, Pallas kernels, local(): pl.pallas_call(functools.partial(last_kernel, seqs=seqs, span=span, nslot...  10.1 us
  transfers between devices with their start and end apart: 44, of which 15 were waited for; matrix products, arithmetic and copies ran while one was open for 7% of the time, Pallas kernels for 30%

commit v1 on v0

--- a/solution.py
+++ b/solution.py
@@ -568,7 +568,7 @@
 
     seqs = 4
     calls = 2
-    steps = seq_count // seqs // calls
+    steps = seq_count // seqs // 4
     all_spec = lambda a, b: pl.BlockSpec((a, b), lambda i, m: (0, 0))
     row_spec = lambda n, w, c=0: pl.BlockSpec((n, w), lambda i, m: (i + c * steps, 0))
     seq_spec = lambda n, a, b, c=0: pl.BlockSpec((n, a, b), lambda i, m: (i + c * steps, 0, 0))
@@ -595,7 +595,7 @@
             ),
             grid_spec=pltpu.PrefetchScalarGridSpec(
                 num_scalar_prefetch=1,
-                grid=(steps,),
+                grid=(seq_count // seqs - steps if c else steps,),
                 in_specs=[
                     row_spec(seqs * span, width, c),
                     all_spec(nshard * total, width),

time: 215 us -> 212 us (0.986)
  waiting for transfers between devices: 32.9 us -> 29.6 us
    ppermute x23, waiting for transfers between devices: 20.5 us -> 17.4 us  [swap(): return lax.ppermute(a, ('rep', 'shard'), perm)]
where the time goes in v1:
time: 212 us; the launch traced here: 211 us
  Pallas kernels  107 us (50%)
  starting transfers between devices  52.4 us (25%)
  waiting for transfers between devices  29.6 us (14%)
  local copies, waits for them, and re-layouts  12.3 us (6%)
  other arithmetic  9 us (4%)
    pallas_call x1, Pallas kernels, local(): pl.pallas_call(functools.partial(ffn_kernel, rps=rps, places=places, nslo...  43.2 us
    ppermute x23, starting transfers between devices, swap(): return lax.ppermute(a, ('rep', 'shard'), perm)  31.2 us
    pallas_call x2, Pallas kernels, back(): pl.pallas_call(functools.partial(back_kernel, seqs=seqs, span=span, begin...  29.9 us
    ppermute x21, starting transfers between devices, send(): return lax.ppermute(a, ('rep', 'shard'), perm)  21.2 us
    pallas_call x2, Pallas kernels, attention(): pl.pallas_call(functools.partial(attend_kernel, sizes=(zs, xs), seqs=seqs...  19.3 us
    ppermute x23, waiting for transfers between devices, swap(): return lax.ppermute(a, ('rep', 'shard'), perm)  17.4 us
    ppermute x21, waiting for transfers between devices, send(): return lax.ppermute(a, ('rep', 'shard'), perm)  12.1 us
    pallas_call x1, Pallas kernels, local(): pl.pallas_call(functools.partial(last_kernel, seqs=seqs, span=span, nslot...  10.1 us
  transfers between devices with their start and end apart: 44, of which 15 were waited for; matrix products, arithmetic and copies ran while one was open for 7% of the time, Pallas kernels for 30%

profile of v1, /device:TPU:0, one launch (start us, length us, event | category | flops | bytes accessed | tf_op | source)
XLA Modules:
  0.0 211.2 jit_solution(12541978439344804241)
XLA Ops:
  0.7 0.9 copy-done
  1.6 3.1 %collective-permute-start = (bf16[64,768]{1,0:T(8,128)(2,1)S(1)}, bf16[64,768]{1,0:T(8,128)(2,1)S(1)}, u32[]{:S(2)}, u32[]{:S(2)}) collective-permute-start(bf16[64,768]{1,0:T(8,128)(2,1)S(1)} %constant_dynamic-slice_fusion.19), channel_id=1, source_target_pairs={{0,2},{1,3},{2,0},{3,1},{4,6},{5,7},{6,4},{7,5},{8,10},{9,11},{10,... | collective-permute-start | bytes 294920 | tf_op jit(solution)/shard_map/ppermute | solution.py:491
  4.7 2.6 %collective-permute-start.1 = (bf16[64,768]{1,0:T(8,128)(2,1)S(1)}, bf16[64,768]{1,0:T(8,128)(2,1)S(1)}, u32[]{:S(2)}, u32[]{:S(2)}) collective-permute-start(bf16[64,768]{1,0:T(8,128)(2,1)S(1)} %constant_dynamic-slice_fusion.19), channel_id=1, source_target_pairs={{0,4},{1,5},{2,6},{3,7},{4,0},{5,1},{6,2},{7,3},{8,12},{9,13},{10,... | collective-permute-start | bytes 294920 | tf_op jit(solution)/shard_map/ppermute | solution.py:491
  7.3 1.2 broadcast_in_dim.6.hidden_ref
  9.1 1.3 stack.43.small_ref
  10.4 4.0 %prep.1 = (f32[25,512]{1,0:T(8,128)}, s32[16,1,128]{2,1,0:T(1,128)}, f32[16,8,128]{2,1,0:T(8,128)}) custom-call(s32[5]{0:T(128)} %stack.37.meta, s32[16,16]{1,0:T(8,128)} %len_ref.3, bf16[2048,512]{1,0:T(8,128)(2,1)} %bitcast.47, bf16[5,64]{1,0:T(8,128)(2,1)} %stack.43.small_ref, bf16[1,256]{1,0:T(2,128)(2,1)} %broadcast_in_dim.6.hidden_ref), custom_call_target="tpu_custom_call" | custom-call | flops 1 | bytes 1 | tf_op jit(solution)/shard_map/prep/pallas_call | solution.py:522
  14.4 0.9 collective-permute-start.7
  15.4 0.7 constant_dynamic-slice_fusion.22
  16.1 0.9 constant_dynamic-slice_fusion.20
  17.0 2.0 collective-permute-done.7
  19.0 0.9 pad_maximum_fusion.9
  19.8 2.5 %collective-permute-start.8 = (f32[50,512]{1,0:T(8,128)S(1)}, f32[50,512]{1,0:T(8,128)S(1)}, u32[]{:S(2)}, u32[]{:S(2)}) collective-permute-start(f32[50,512]{1,0:T(8,128)S(1)} %pad_maximum_fusion.9), channel_id=1, source_target_pairs={{0,4},{1,5},{2,6},{3,7},{4,0},{5,1},{6,2},{7,3},{8,12},{9,13},{10,... | collective-permute-start | bytes 307208 | tf_op jit(solution)/shard_map/ppermute | solution.py:491
  22.3 2.1 collective-permute-start.3
  24.4 2.4 %collective-permute-start.5 = (bf16[64,1152]{1,0:T(8,128)(2,1)S(1)}, bf16[64,1152]{1,0:T(8,128)(2,1)S(1)}, u32[]{:S(2)}, u32[]{:S(2)}) collective-permute-start(bf16[64,1152]{1,0:T(8,128)(2,1)S(1)} %pad_maximum_fusion.7), channel_id=1, source_target_pairs={{0,6},{1,7},{2,4},{3,5},{4,2},{5,3},{6,0},{7,1},{8,14},{9,15},{10,... | collective-permute-start | bytes 442376 | tf_op jit(solution)/shard_map/ppermute | solution.py:491
  26.8 1.5 collective-permute-start.10
  28.3 0.9 collective-permute-done.8
  29.2 2.5 %collective-permute-start.9 = (f32[100,512]{1,0:T(8,128)S(1)}, f32[100,512]{1,0:T(8,128)S(1)}, u32[]{:S(2)}, u32[]{:S(2)}) collective-permute-start(f32[100,512]{1,0:T(8,128)S(1)} %pad_maximum_fusion.6), channel_id=1, source_target_pairs={{0,1},{1,0},{2,3},{3,2},{4,5},{5,4},{6,7},{7,6},{8,9},{9,8},{10,11... | collective-permute-start | bytes 614408 | tf_op jit(solution)/shard_map/ppermute | solution.py:491
  31.7 5.0 %collective-permute-done.4 = bf16[64,1152]{1,0:T(8,128)(2,1)S(1)} collective-permute-done((bf16[64,1152]{1,0:T(8,128)(2,1)S(1)}, bf16[64,1152]{1,0:T(8,128)(2,1)S(1)}, u32[]{:S(2)}, u32[]{:S(2)}) %collective-permute-start.4) | collective-permute-done | bytes 147488 | tf_op jit(solution)/shard_map/ppermute | solution.py:491
  36.9 2.0 collective-permute-start.13
  39.0 1.5 collective-permute-start.6
  40.5 0.8 pad_maximum_fusion.3.refs_1_.refs_3_.refs_6_.slots_ref
  41.3 0.7 copy-done.16
  42.2 7.0 %attention.2 = (bf16[512,1536]{1,0:T(8,128)(2,1)}, bf16[2048,1536]{1,0:T(8,128)(2,1)}, bf16[2048,512]{1,0:T(8,128)(2,1)}, f32[16,4,256]{2,1,0:T(4,128)}) custom-call(s32[5]{0:T(128)} %stack.37.meta, bf16[2048,512]{1,0:T(8,128)(2,1)} %bitcast.48, f32[200,512]{1,0:T(8,128)} %pad_maximum_fusion.3.refs_1_.refs_3_.refs_6_.slots_ref, ...), custom_call_target="tpu_custom_call" | custom-call | flops 1 | bytes 1 | tf_op jit(solution)/shard_map/attention/pallas_call | solution.py:587
  49.3 0.6 collective-permute-start.17
  49.9 1.5 collective-permute-start.16
  52.0 12.3 %attention.3 = (bf16[2048,1536]{1,0:T(8,128)(2,1)}, bf16[2048,512]{1,0:T(8,128)(2,1)}, f32[16,4,256]{2,1,0:T(4,128)}) custom-call(s32[5]{0:T(128)} %stack.37.meta, bf16[2048,512]{1,0:T(8,128)(2,1)} %bitcast.49, f32[200,512]{1,0:T(8,128)} %pad_maximum_fusion.3.refs_1_.refs_3_.refs_6_.slots_ref, ...), custom_call_target="tpu_custom_call", output_to_operand_aliasing={{0}: (6, {}), {1}: (7, {}), {2}: (8, {})} | custom-call | flops 1 | bytes 1 | tf_op jit(solution)/shard_map/attention/pallas_call | solution.py:587
  65.4 1.5 collective-permute-done.18.refs_10_
  66.9 0.8 collective-permute-done.19.refs_11_
  67.8 0.8 copy-done.13
  68.6 43.2 %ffn.1 = (f32[2048,512]{1,0:T(8,128)}, f32[2048,512]{1,0:T(8,128)}, bf16[512,2304]{1,0:T(8,128)(2,1)}, bf16[512,2304]{1,0:T(8,128)(2,1)}, bf16[512,512]{1,0:T(8,128)(2,1)}, /*index=5*/f32[8,2048]{1,0:T(8,128)}) custom-call(s32[5]{0:T(128)} %stack.37.meta, bf16[2048,512]{1,0:T(8,128)(2,1)} %get-tuple-element.64.refs_0_, bf16[2048,512]{1,0:T(8,128)(2,1)} %bitcast.50, ...), custom_call_target="tpu_custom_call" | custom-call | flops 1 | bytes 1 | tf_op jit(solution)/shard_map/ffn/pallas_call | solution.py:649
  112.1 14.0 %back.2 = (bf16[2048,1536]{1,0:T(8,128)(2,1)}, bf16[16,16,512]{2,1,0:T(8,128)(2,1)}, f32[520,1536]{1,0:T(8,128)}) custom-call(s32[5]{0:T(128)} %stack.37.meta, f32[2048,512]{1,0:T(8,128)} %get-tuple-element.83.refs_0_.dr_ref, bf16[2048,512]{1,0:T(8,128)(2,1)} %bitcast.51, bf16[2048,1536]{1,0:T(8,128)(2,1)} %get-tuple-element.72.refs_2_, ...), custom_call_target="tpu_custom_call" | custom-call | flops 1 | bytes 1 | tf_op jit(solution)/shard_map/back/pallas_call | solution.py:754
  127.4 0.8 convert.38
  128.4 1.6 collective-permute-start.21
  130.0 15.9 %back.3 = (bf16[2048,1536]{1,0:T(8,128)(2,1)}, bf16[16,16,512]{2,1,0:T(8,128)(2,1)}, bf16[512,768]{1,0:T(8,128)(2,1)}, bf16[512,768]{1,0:T(8,128)(2,1)}, f32[8,512]{1,0:T(8,128)}) custom-call(s32[5]{0:T(128)} %stack.37.meta, f32[2048,512]{1,0:T(8,128)} %get-tuple-element.83.refs_0_.dr_ref, ...), custom_call_target="tpu_custom_call", output_to_operand_aliasing={{0}: (11, {}), {1}: (12, {})} | custom-call | flops 1 | bytes 1 | tf_op jit(solution)/shard_map/back/pallas_call | solution.py:754
  145.9 0.7 slice.295
  147.0 0.6 copy-done.7
  148.4 4.2 %collective-permute-done.24 = bf16[1,4,25,512]{3,1,2,0:T(4,128)(2,1)S(1)} collective-permute-done((bf16[1,4,25,512]{3,1,2,0:T(4,128)(2,1)S(1)}, bf16[1,4,25,512]{3,1,2,0:T(4,128)(2,1)S(1)}, u32[]{:S(2)}, u32[]{:S(2)}) %collective-permute-start.24) | collective-permute-done | bytes 102432 | tf_op jit(solution)/shard_map/ppermute | solution.py:491
  152.7 4.3 %collective-permute-start.25 = (bf16[2,25,512]{2,0,1:T(2,128)(2,1)S(1)}, bf16[2,25,512]{2,0,1:T(2,128)(2,1)S(1)}, u32[]{:S(2)}, u32[]{:S(2)}) collective-permute-start(bf16[2,25,512]{2,0,1:T(2,128)(2,1)S(1)} %slice_bitcast_fusion.1), channel_id=1, source_target_pairs={{0,4},{1,5},{2,6},{3,7},{4,0},{5,1},{6,2},{7,3},{8,12},{9,13},{10,... | collective-permute-start | bytes 153608 | tf_op jit(solution)/shard_map/ppermute | solution.py:491
  157.1 2.4 %collective-permute-done.25 = bf16[2,25,512]{2,0,1:T(2,128)(2,1)S(1)} collective-permute-done((bf16[2,25,512]{2,0,1:T(2,128)(2,1)S(1)}, bf16[2,25,512]{2,0,1:T(2,128)(2,1)S(1)}, u32[]{:S(2)}, u32[]{:S(2)}) %collective-permute-start.25) | collective-permute-done | bytes 51232 | tf_op jit(solution)/shard_map/ppermute | solution.py:491
  159.6 2.1 %collective-permute-start.26 = (bf16[1,25,512]{2,0,1:T(2,128)(2,1)S(1)}, bf16[1,25,512]{2,0,1:T(2,128)(2,1)S(1)}, u32[]{:S(2)}, u32[]{:S(2)}) collective-permute-start(bf16[1,25,512]{2,0,1:T(2,128)(2,1)S(1)} %slice.237), channel_id=1, source_target_pairs={{0,2},{1,3},{2,0},{3,1},{4,6},{5,7},{6,4},{7,5},{8,10},{9,11},{10,... | collective-permute-start | bytes 76808 | tf_op jit(solution)/shard_map/ppermute | solution.py:491
  161.8 0.9 collective-permute-start.36
  162.7 1.4 collective-permute-start.37
  164.8 0.6 slice_bitcast_fusion.3.dpool_ref
  165.4 1.3 add_convert_fusion.1
  166.9 1.4 collective-permute-start.27
  168.3 0.6 collective-permute-start.28
  168.9 1.5 collective-permute-start.29
  170.4 10.1 %last.1 = f32[2048,512]{1,0:T(8,128)} custom-call(s32[5]{0:T(128)} %stack.37.meta, s32[16,16]{1,0:T(8,128)} %len_ref.3, f32[2048,512]{1,0:T(8,128)} %get-tuple-element.83.refs_0_.dr_ref, bf16[2048,512]{1,0:T(8,128)(2,1)} %bitcast.53, bf16[2048,1536]{1,0:T(8,128)(2,1)} %get-tuple-element.84.dqkv_ref, bf16[512,1536]{1,0:T(8,128)(2,1)} %get-tuple-element.61.refs_4_.w_ref, ...), custom_call_target="tpu_custom_call" | custom-call | flops 1 | bytes 1 | tf_op jit(solution)/shard_map/last/pallas_call | solution.py:834
  181.0 1.9 collective-permute-start.30
  182.9 2.9 %collective-permute-start.31 = (bf16[64,384]{1,0:T(8,128)(2,1)S(1)}, bf16[64,384]{1,0:T(8,128)(2,1)S(1)}, u32[]{:S(2)}, u32[]{:S(2)}) collective-permute-start(bf16[64,384]{1,0:T(8,128)(2,1)S(1)} %get-tuple-element.116), channel_id=1, source_target_pairs={{0,4},{1,5},{2,6},{3,7},{4,0},{5,1},{6,2},{7,3},{8,12},{9,13},{10,... | collective-permute-start | bytes 147464 | tf_op jit(solution)/shard_map/ppermute | solution.py:502
  185.8 1.1 collective-permute-start.32
  186.9 1.0 collective-permute-start.38
  188.0 2.8 %collective-permute-start.40 = (bf16[64,1152]{1,0:T(8,128)(2,1)S(1)}, bf16[64,1152]{1,0:T(8,128)(2,1)S(1)}, u32[]{:S(2)}, u32[]{:S(2)}) collective-permute-start(bf16[64,1152]{1,0:T(8,128)(2,1)S(1)} %get-tuple-element.98), channel_id=1, source_target_pairs={{0,6},{1,7},{2,0},{3,1},{4,2},{5,3},{6,4},{7,5},{8,14},{9,15},{10,... | collective-permute-start | bytes 442376 | tf_op jit(solution)/shard_map/ppermute | solution.py:502
  190.8 1.2 collective-permute-done.31
  192.1 1.4 collective-permute-start.34
  193.5 1.2 collective-permute-done.38
  194.7 4.6 %collective-permute-done.39 = bf16[64,1152]{1,0:T(8,128)(2,1)S(1)} collective-permute-done((bf16[64,1152]{1,0:T(8,128)(2,1)S(1)}, bf16[64,1152]{1,0:T(8,128)(2,1)S(1)}, u32[]{:S(2)}, u32[]{:S(2)}) %collective-permute-start.39) | collective-permute-done | bytes 147488 | tf_op jit(solution)/shard_map/ppermute | solution.py:502
  199.5 1.4 collective-permute-start.42
  202.1 0.8 pad_maximum_fusion.5
  203.5 2.1 %collective-permute-done.41 = bf16[64,1152]{1,0:T(8,128)(2,1)S(1)} collective-permute-done((bf16[64,1152]{1,0:T(8,128)(2,1)S(1)}, bf16[64,1152]{1,0:T(8,128)(2,1)S(1)}, u32[]{:S(2)}, u32[]{:S(2)}) %collective-permute-start.41) | collective-permute-done | bytes 147488 | tf_op jit(solution)/shard_map/ppermute | solution.py:502
  205.6 2.9 %collective-permute-done.42 = bf16[64,1152]{1,0:T(8,128)(2,1)S(1)} collective-permute-done((bf16[64,1152]{1,0:T(8,128)(2,1)S(1)}, bf16[64,1152]{1,0:T(8,128)(2,1)S(1)}, u32[]{:S(2)}, u32[]{:S(2)}) %collective-permute-start.42) | collective-permute-done | bytes 147488 | tf_op jit(solution)/shard_map/ppermute | solution.py:502
  208.8 0.8 fusion
  209.7 0.7 pad_maximum_fusion.8
  210.3 0.9 maximum_maximum_fusion
  (153 shorter events, 9.6 us)
Async XLA Ops:
  0.6 0.9 copy-start
  1.6 20.7 %collective-permute-start = (bf16[64,768]{1,0:T(8,128)(2,1)S(1)}, bf16[64,768]{1,0:T(8,128)(2,1)S(1)}, u32[]{:S(2)}, u32[]{:S(2)}) collective-permute-start(bf16[64,768]{1,0:T(8,128)(2,1)S(1)} %constant_dynamic-slice_fusion.19), channel_id=1, source_target_pairs={{0,2},{1,3},{2,0},{3,1},{4,6},{5,7},{6,4},{7,5},{8,10},{9,11},{10,... | collective-permute-start | bytes 294920 | tf_op jit(solution)/shard_map/ppermute | solution.py:491
  4.7 17.6 %collective-permute-start.1 = (bf16[64,768]{1,0:T(8,128)(2,1)S(1)}, bf16[64,768]{1,0:T(8,128)(2,1)S(1)}, u32[]{:S(2)}, u32[]{:S(2)}) collective-permute-start(bf16[64,768]{1,0:T(8,128)(2,1)S(1)} %constant_dynamic-slice_fusion.19), channel_id=1, source_target_pairs={{0,4},{1,5},{2,6},{3,7},{4,0},{5,1},{6,2},{7,3},{8,12},{9,13},{10,... | collective-permute-start | bytes 294920 | tf_op jit(solution)/shard_map/ppermute | solution.py:491
  7.3 15.0 %collective-permute-start.2 = (bf16[64,768]{1,0:T(8,128)(2,1)S(1)}, bf16[64,768]{1,0:T(8,128)(2,1)S(1)}, u32[]{:S(2)}, u32[]{:S(2)}) collective-permute-start(bf16[64,768]{1,0:T(8,128)(2,1)S(1)} %constant_dynamic-slice_fusion.19), channel_id=1, source_target_pairs={{0,6},{1,7},{2,4},{3,5},{4,2},{5,3},{6,0},{7,1},{8,14},{9,15},{10,... | collective-permute-start | bytes 294920 | tf_op jit(solution)/shard_map/ppermute | solution.py:491
  14.4 14.8 %copy-start.14 = (f32[25,512]{1,0:T(8,128)S(1)}, f32[25,512]{1,0:T(8,128)}, u32[]{:S(2)}) copy-start(f32[25,512]{1,0:T(8,128)} %get-tuple-element.52) | copy-start | bytes 153604
  14.4 4.5 %collective-permute-start.7 = (f32[25,512]{1,0:T(8,128)}, f32[25,512]{1,0:T(8,128)S(1)}, u32[]{:S(2)}, u32[]{:S(2)}) collective-permute-start(f32[25,512]{1,0:T(8,128)} %get-tuple-element.52), channel_id=1, source_target_pairs={{0,2},{1,3},{2,0},{3,1},{4,6},{5,7},{6,4},{7,5},{8,10},{9,11},{10,... | collective-permute-start | bytes 153608 | tf_op jit(solution)/shard_map/ppermute | solution.py:491
  19.8 9.4 %collective-permute-start.8 = (f32[50,512]{1,0:T(8,128)S(1)}, f32[50,512]{1,0:T(8,128)S(1)}, u32[]{:S(2)}, u32[]{:S(2)}) collective-permute-start(f32[50,512]{1,0:T(8,128)S(1)} %pad_maximum_fusion.9), channel_id=1, source_target_pairs={{0,4},{1,5},{2,6},{3,7},{4,0},{5,1},{6,2},{7,3},{8,12},{9,13},{10,... | collective-permute-start | bytes 307208 | tf_op jit(solution)/shard_map/ppermute | solution.py:491
  22.3 19.0 %copy-start.3 = (bf16[256,768]{1,0:T(8,128)(2,1)}, bf16[256,768]{1,0:T(8,128)(2,1)S(1)}, u32[]{:S(2)}) copy-start(bf16[256,768]{1,0:T(8,128)(2,1)S(1)} %pad_maximum_fusion.4.refs_4_) | copy-start | bytes 1179652
  22.3 6.9 %collective-permute-start.3 = (bf16[64,1152]{1,0:T(8,128)(2,1)S(1)}, bf16[64,1152]{1,0:T(8,128)(2,1)S(1)}, u32[]{:S(2)}, u32[]{:S(2)}) collective-permute-start(bf16[64,1152]{1,0:T(8,128)(2,1)S(1)} %pad_maximum_fusion.7), channel_id=1, source_target_pairs={{0,2},{1,3},{2,0},{3,1},{4,6},{5,7},{6,4},{7,5},{8,10},{9,11},{10,... | collective-permute-start | bytes 442376 | tf_op jit(solution)/shard_map/ppermute | solution.py:491
  24.4 12.3 %collective-permute-start.4 = (bf16[64,1152]{1,0:T(8,128)(2,1)S(1)}, bf16[64,1152]{1,0:T(8,128)(2,1)S(1)}, u32[]{:S(2)}, u32[]{:S(2)}) collective-permute-start(bf16[64,1152]{1,0:T(8,128)(2,1)S(1)} %pad_maximum_fusion.7), channel_id=1, source_target_pairs={{0,4},{1,5},{2,6},{3,7},{4,0},{5,1},{6,2},{7,3},{8,12},{9,13},{10,... | collective-permute-start | bytes 442376 | tf_op jit(solution)/shard_map/ppermute | solution.py:491
  24.4 12.3 %collective-permute-start.5 = (bf16[64,1152]{1,0:T(8,128)(2,1)S(1)}, bf16[64,1152]{1,0:T(8,128)(2,1)S(1)}, u32[]{:S(2)}, u32[]{:S(2)}) collective-permute-start(bf16[64,1152]{1,0:T(8,128)(2,1)S(1)} %pad_maximum_fusion.7), channel_id=1, source_target_pairs={{0,6},{1,7},{2,4},{3,5},{4,2},{5,3},{6,0},{7,1},{8,14},{9,15},{10,... | collective-permute-start | bytes 442376 | tf_op jit(solution)/shard_map/ppermute | solution.py:491
  26.8 9.9 %collective-permute-start.10 = (bf16[256,768]{1,0:T(8,128)(2,1)S(1)}, bf16[256,768]{1,0:T(8,128)(2,1)S(1)}, u32[]{:S(2)}, u32[]{:S(2)}) collective-permute-start(bf16[256,768]{1,0:T(8,128)(2,1)S(1)} %pad_maximum_fusion.4.refs_4_), channel_id=1, source_target_pairs={{0,1},{1,0},{2,3},{3,2},{4,5},{5,4},{6,7},{7,6},{8,9},{9,8},{10,11... | collective-permute-start | bytes 1179656 | tf_op jit(solution)/shard_map/ppermute | solution.py:491
  29.2 12.1 %collective-permute-start.11 = (bf16[256,768]{1,0:T(8,128)(2,1)S(1)}, bf16[256,768]{1,0:T(8,128)(2,1)S(1)}, u32[]{:S(2)}, u32[]{:S(2)}) collective-permute-start(bf16[256,768]{1,0:T(8,128)(2,1)S(1)} %pad_maximum_fusion.4.refs_4_), channel_id=1, source_target_pairs={{0,8},{1,9},{2,10},{3,11},{4,12},{5,13},{6,14},{7,15},{8,0},{9,1},... | collective-permute-start | bytes 1179656 | tf_op jit(solution)/shard_map/ppermute | solution.py:491
  29.2 11.2 %collective-permute-start.9 = (f32[100,512]{1,0:T(8,128)S(1)}, f32[100,512]{1,0:T(8,128)S(1)}, u32[]{:S(2)}, u32[]{:S(2)}) collective-permute-start(f32[100,512]{1,0:T(8,128)S(1)} %pad_maximum_fusion.6), channel_id=1, source_target_pairs={{0,1},{1,0},{2,3},{3,2},{4,5},{5,4},{6,7},{7,6},{8,9},{9,8},{10,11... | collective-permute-start | bytes 614408 | tf_op jit(solution)/shard_map/ppermute | solution.py:491
  36.8 4.5 %copy-start.15 = (bf16[256,768]{1,0:T(8,128)(2,1)}, bf16[256,768]{1,0:T(8,128)(2,1)S(1)}, u32[]{:S(2)}) copy-start(bf16[256,768]{1,0:T(8,128)(2,1)S(1)} %collective-permute-done.10.refs_5_) | copy-start | bytes 1179652
  36.8 4.5 %collective-permute-start.12 = (bf16[256,768]{1,0:T(8,128)(2,1)S(1)}, bf16[256,768]{1,0:T(8,128)(2,1)S(1)}, u32[]{:S(2)}, u32[]{:S(2)}) collective-permute-start(bf16[256,768]{1,0:T(8,128)(2,1)S(1)} %collective-permute-done.10.refs_5_), channel_id=1, source_target_pairs={{0,8},{1,9},{2,10},{3,11},{4,12},{5,13},{6,14},{7,15},{8,0},{9,1},... | collective-permute-start | bytes 1179656 | tf_op jit(solution)/shard_map/ppermute | solution.py:491
  36.9 12.3 %collective-permute-start.13 = (bf16[128,1152]{1,0:T(8,128)(2,1)S(1)}, bf16[128,1152]{1,0:T(8,128)(2,1)S(1)}, u32[]{:S(2)}, u32[]{:S(2)}) collective-permute-start(bf16[128,1152]{1,0:T(8,128)(2,1)S(1)} %bitcast.63), channel_id=1, source_target_pairs={{0,16},{1,17},{2,18},{3,19},{4,20},{5,21},{6,22},{7,23},{8,24},{9,... | collective-permute-start | bytes 884744 | tf_op jit(solution)/shard_map/ppermute | solution.py:491
  39.0 10.3 %collective-permute-start.6 = (bf16[128,1152]{1,0:T(8,128)(2,1)S(1)}, bf16[128,1152]{1,0:T(8,128)(2,1)S(1)}, u32[]{:S(2)}, u32[]{:S(2)}) collective-permute-start(bf16[128,1152]{1,0:T(8,128)(2,1)S(1)} %bitcast.61), channel_id=1, source_target_pairs={{0,1},{1,0},{2,3},{3,2},{4,5},{5,4},{6,7},{7,6},{8,9},{9,8},{10,11... | collective-permute-start | bytes 884744 | tf_op jit(solution)/shard_map/ppermute | solution.py:491
  41.3 0.7 copy-start.16
  41.3 0.9 copy-start.17
  49.3 15.0 %copy-start.5 = (bf16[256,1152]{1,0:T(8,128)(2,1)}, bf16[256,1152]{1,0:T(8,128)(2,1)S(1)}, u32[]{:S(2)}) copy-start(bf16[256,1152]{1,0:T(8,128)(2,1)S(1)} %constant_dynamic-update-slice_fusion.2.refs_5_) | copy-start | bytes 1769476
  49.3 15.2 %collective-permute-start.17 = (bf16[256,1152]{1,0:T(8,128)(2,1)S(1)}, bf16[256,1152]{1,0:T(8,128)(2,1)S(1)}, u32[]{:S(2)}, u32[]{:S(2)}) collective-permute-start(bf16[256,1152]{1,0:T(8,128)(2,1)S(1)} %constant_dynamic-update-slice_fusion.2.refs_5_), channel_id=1, source_target_pairs={{0,1},{1,0},{2,3},{3,2},{4,5},{5,4},{6,7},{7,6},{8,9},{9,8},{10,11... | collective-permute-start | bytes 1769480 | tf_op jit(solution)/shard_map/ppermute | solution.py:491
  49.9 14.3 %copy-start.4 = (bf16[256,1152]{1,0:T(8,128)(2,1)}, bf16[256,1152]{1,0:T(8,128)(2,1)S(1)}, u32[]{:S(2)}) copy-start(bf16[256,1152]{1,0:T(8,128)(2,1)S(1)} %constant_dynamic-update-slice_fusion.refs_4_) | copy-start | bytes 1769476
  49.9 14.9 %collective-permute-start.16 = (bf16[256,1152]{1,0:T(8,128)(2,1)S(1)}, bf16[256,1152]{1,0:T(8,128)(2,1)S(1)}, u32[]{:S(2)}, u32[]{:S(2)}) collective-permute-start(bf16[256,1152]{1,0:T(8,128)(2,1)S(1)} %constant_dynamic-update-slice_fusion.refs_4_), channel_id=1, source_target_pairs={{0,16},{1,17},{2,18},{3,19},{4,20},{5,21},{6,22},{7,23},{8,24},{9,... | collective-permute-start | bytes 1769480 | tf_op jit(solution)/shard_map/ppermute | solution.py:491
  51.4 14.0 %collective-permute-start.15 = (bf16[256,1152]{1,0:T(8,128)(2,1)S(1)}, bf16[256,1152]{1,0:T(8,128)(2,1)S(1)}, u32[]{:S(2)}, u32[]{:S(2)}) collective-permute-start(bf16[256,1152]{1,0:T(8,128)(2,1)S(1)} %constant_dynamic-update-slice_fusion.2.refs_5_), channel_id=1, source_target_pairs={{0,8},{1,9},{2,10},{3,11},{4,12},{5,13},{6,14},{7,15},{8,0},{9,1},... | collective-permute-start | bytes 1769480 | tf_op jit(solution)/shard_map/ppermute | solution.py:491
  51.4 14.0 %collective-permute-start.14 = (bf16[256,1152]{1,0:T(8,128)(2,1)S(1)}, bf16[256,1152]{1,0:T(8,128)(2,1)S(1)}, u32[]{:S(2)}, u32[]{:S(2)}) collective-permute-start(bf16[256,1152]{1,0:T(8,128)(2,1)S(1)} %constant_dynamic-update-slice_fusion.refs_4_), channel_id=1, source_target_pairs={{0,8},{1,9},{2,10},{3,11},{4,12},{5,13},{6,14},{7,15},{8,0},{9,1},... | collective-permute-start | bytes 1769480 | tf_op jit(solution)/shard_map/ppermute | solution.py:491
  64.5 3.2 %copy-start.8 = (bf16[256,1152]{1,0:T(8,128)(2,1)}, bf16[256,1152]{1,0:T(8,128)(2,1)S(1)}, u32[]{:S(2)}) copy-start(bf16[256,1152]{1,0:T(8,128)(2,1)S(1)} %collective-permute-done.17.refs_9_) | copy-start | bytes 1769476
  64.9 2.9 %copy-start.9 = (bf16[256,1152]{1,0:T(8,128)(2,1)}, bf16[256,1152]{1,0:T(8,128)(2,1)S(1)}, u32[]{:S(2)}) copy-start(bf16[256,1152]{1,0:T(8,128)(2,1)S(1)} %collective-permute-done.16.refs_8_) | copy-start | bytes 1769476
  64.9 2.0 collective-permute-start.18
  64.9 2.8 %collective-permute-start.19 = (bf16[256,1152]{1,0:T(8,128)(2,1)S(1)}, bf16[256,1152]{1,0:T(8,128)(2,1)S(1)}, u32[]{:S(2)}, u32[]{:S(2)}) collective-permute-start(bf16[256,1152]{1,0:T(8,128)(2,1)S(1)} %collective-permute-done.17.refs_9_), channel_id=1, source_target_pairs={{0,8},{1,9},{2,10},{3,11},{4,12},{5,13},{6,14},{7,15},{8,0},{9,1},... | collective-permute-start | bytes 1769480 | tf_op jit(solution)/shard_map/ppermute | solution.py:491
  65.4 2.3 %copy-start.10 = (bf16[256,1152]{1,0:T(8,128)(2,1)}, bf16[256,1152]{1,0:T(8,128)(2,1)S(1)}, u32[]{:S(2)}) copy-start(bf16[256,1152]{1,0:T(8,128)(2,1)S(1)} %collective-permute-done.15.refs_7_) | copy-start | bytes 1769476
  65.4 2.3 %copy-start.11 = (bf16[256,1152]{1,0:T(8,128)(2,1)}, bf16[256,1152]{1,0:T(8,128)(2,1)S(1)}, u32[]{:S(2)}) copy-start(bf16[256,1152]{1,0:T(8,128)(2,1)S(1)} %collective-permute-done.14.refs_6_) | copy-start | bytes 1769476
  66.9 0.9 copy-start.12
  67.7 0.9 copy-start.13
  111.8 14.3 %collective-permute-start.20 = (bf16[512,2304]{1,0:T(8,128)(2,1)}, bf16[512,2304]{1,0:T(8,128)(2,1)S(1)}, u32[]{:S(2)}, u32[]{:S(2)}) collective-permute-start(bf16[512,2304]{1,0:T(8,128)(2,1)} %get-tuple-element.71), channel_id=1, source_target_pairs={{0,8},{1,9},{2,10},{3,11},{4,12},{5,13},{6,14},{7,15},{8,0},{9,1},... | collective-permute-start | bytes 7077896 | tf_op jit(solution)/shard_map/ppermute | solution.py:502
  112.1 14.1 %copy-start.2 = (bf16[512,2304]{1,0:T(8,128)(2,1)S(1)}, bf16[512,2304]{1,0:T(8,128)(2,1)}, u32[]{:S(2)}) copy-start(bf16[512,2304]{1,0:T(8,128)(2,1)} %get-tuple-element.70) | copy-start | bytes 7077892
  127.0 19.7 %collective-permute-start.22 = (bf16[4,2,32,1152]{3,2,1,0:T(8,128)(2,1)S(1)}, bf16[4,2,32,1152]{3,2,1,0:T(8,128)(2,1)S(1)}, u32[]{:S(2)}, u32[]{:S(2)}) collective-permute-start(bf16[4,2,32,1152]{3,2,1,0:T(8,128)(2,1)S(1)} %constant_dynamic-slice_fusion.17), channel_id=1, source_target_pairs={{0,16},{1,17},{2,18},{3,19},{4,20},{5,21},{6,22},{7,23},{8,24},{9,... | collective-permute-start | bytes 1769480 | tf_op jit(solution)/shard_map/ppermute | solution.py:502
  128.4 18.4 %collective-permute-start.21 = (bf16[4,1,32,2304]{3,2,1,0:T(8,128)(2,1)S(1)}, bf16[4,1,32,2304]{3,2,1,0:T(8,128)(2,1)S(1)}, u32[]{:S(2)}, u32[]{:S(2)}) collective-permute-start(bf16[4,1,32,2304]{3,2,1,0:T(8,128)(2,1)S(1)} %constant_dynamic-slice_fusion.18), channel_id=1, source_target_pairs={{0,1},{1,0},{2,3},{3,2},{4,5},{5,4},{6,7},{7,6},{8,9},{9,8},{10,11... | collective-permute-start | bytes 1769480 | tf_op jit(solution)/shard_map/ppermute | solution.py:502
  146.6 1.0 copy-start.7
  147.6 17.8 %copy-start.6 = (bf16[512,768]{1,0:T(8,128)(2,1)S(1)}, bf16[512,768]{1,0:T(8,128)(2,1)}, u32[]{:S(2)}) copy-start(bf16[512,768]{1,0:T(8,128)(2,1)} %get-tuple-element.81) | copy-start | bytes 2359300
  147.9 4.7 %collective-permute-start.24 = (bf16[1,4,25,512]{3,1,2,0:T(4,128)(2,1)S(1)}, bf16[1,4,25,512]{3,1,2,0:T(4,128)(2,1)S(1)}, u32[]{:S(2)}, u32[]{:S(2)}) collective-permute-start(bf16[1,4,25,512]{3,1,2,0:T(4,128)(2,1)S(1)} %pad_maximum_fusion.10), channel_id=1, source_target_pairs={{0,1},{1,0},{2,3},{3,2},{4,5},{5,4},{6,7},{7,6},{8,9},{9,8},{10,11... | collective-permute-start | bytes 307208 | tf_op jit(solution)/shard_map/ppermute | solution.py:491
  148.4 17.1 %collective-permute-start.23 = (bf16[512,768]{1,0:T(8,128)(2,1)}, bf16[512,768]{1,0:T(8,128)(2,1)}, u32[]{:S(2)}, u32[]{:S(2)}) collective-permute-start(bf16[512,768]{1,0:T(8,128)(2,1)} %get-tuple-element.82), channel_id=1, source_target_pairs={{0,8},{1,9},{2,10},{3,11},{4,12},{5,13},{6,14},{7,15},{8,0},{9,1},... | collective-permute-start | bytes 2359304 | tf_op jit(solution)/shard_map/ppermute | solution.py:502
  152.7 6.8 %collective-permute-start.25 = (bf16[2,25,512]{2,0,1:T(2,128)(2,1)S(1)}, bf16[2,25,512]{2,0,1:T(2,128)(2,1)S(1)}, u32[]{:S(2)}, u32[]{:S(2)}) collective-permute-start(bf16[2,25,512]{2,0,1:T(2,128)(2,1)S(1)} %slice_bitcast_fusion.1), channel_id=1, source_target_pairs={{0,4},{1,5},{2,6},{3,7},{4,0},{5,1},{6,2},{7,3},{8,12},{9,13},{10,... | collective-permute-start | bytes 153608 | tf_op jit(solution)/shard_map/ppermute | solution.py:491
  159.6 4.4 %collective-permute-start.26 = (bf16[1,25,512]{2,0,1:T(2,128)(2,1)S(1)}, bf16[1,25,512]{2,0,1:T(2,128)(2,1)S(1)}, u32[]{:S(2)}, u32[]{:S(2)}) collective-permute-start(bf16[1,25,512]{2,0,1:T(2,128)(2,1)S(1)} %slice.237), channel_id=1, source_target_pairs={{0,2},{1,3},{2,0},{3,1},{4,6},{5,7},{6,4},{7,5},{8,10},{9,11},{10,... | collective-permute-start | bytes 76808 | tf_op jit(solution)/shard_map/ppermute | solution.py:491
  161.8 18.8 %collective-permute-start.36 = (bf16[4,1,32,1152]{3,2,1,0:T(8,128)(2,1)S(1)}, bf16[4,1,32,1152]{3,2,1,0:T(8,128)(2,1)S(1)}, u32[]{:S(2)}, u32[]{:S(2)}) collective-permute-start(bf16[4,1,32,1152]{3,2,1,0:T(8,128)(2,1)S(1)} %constant_dynamic-slice_fusion.4), channel_id=1, source_target_pairs={{0,16},{1,17},{2,18},{3,19},{4,20},{5,21},{6,22},{7,23},{8,24},{9,... | collective-permute-start | bytes 884744 | tf_op jit(solution)/shard_map/ppermute | solution.py:502
  162.7 18.0 %collective-permute-start.37 = (bf16[4,1,32,1152]{3,2,1,0:T(8,128)(2,1)S(1)}, bf16[4,1,32,1152]{3,2,1,0:T(8,128)(2,1)S(1)}, u32[]{:S(2)}, u32[]{:S(2)}) collective-permute-start(bf16[4,1,32,1152]{3,2,1,0:T(8,128)(2,1)S(1)} %constant_dynamic-slice_fusion.3), channel_id=1, source_target_pairs={{0,1},{1,0},{2,3},{3,2},{4,5},{5,4},{6,7},{7,6},{8,9},{9,8},{10,11... | collective-permute-start | bytes 884744 | tf_op jit(solution)/shard_map/ppermute | solution.py:502
  166.9 13.9 %collective-permute-start.27 = (bf16[256,384]{1,0:T(8,128)(2,1)S(1)}, bf16[256,384]{1,0:T(8,128)(2,1)S(1)}, u32[]{:S(2)}, u32[]{:S(2)}) collective-permute-start(bf16[256,384]{1,0:T(8,128)(2,1)S(1)} %bitcast.68), channel_id=1, source_target_pairs={{0,16},{1,17},{2,18},{3,19},{4,20},{5,21},{6,22},{7,23},{8,24},{9,... | collective-permute-start | bytes 589832 | tf_op jit(solution)/shard_map/ppermute | solution.py:502
  168.3 12.5 %collective-permute-start.28 = (bf16[256,384]{1,0:T(8,128)(2,1)S(1)}, bf16[256,384]{1,0:T(8,128)(2,1)S(1)}, u32[]{:S(2)}, u32[]{:S(2)}) collective-permute-start(bf16[256,384]{1,0:T(8,128)(2,1)S(1)} %bitcast.67), channel_id=1, source_target_pairs={{0,1},{1,0},{2,3},{3,2},{4,5},{5,4},{6,7},{7,6},{8,9},{9,8},{10,11... | collective-permute-start | bytes 589832 | tf_op jit(solution)/shard_map/ppermute | solution.py:502
  168.9 11.9 %collective-permute-start.29 = (bf16[256,384]{1,0:T(8,128)(2,1)S(1)}, bf16[256,384]{1,0:T(8,128)(2,1)S(1)}, u32[]{:S(2)}, u32[]{:S(2)}) collective-permute-start(bf16[256,384]{1,0:T(8,128)(2,1)S(1)} %bitcast.66), channel_id=1, source_target_pairs={{0,17},{1,16},{2,19},{3,18},{4,21},{5,20},{6,23},{7,22},{8,25},{9,... | collective-permute-start | bytes 589832 | tf_op jit(solution)/shard_map/ppermute | solution.py:502
  181.0 7.0 %collective-permute-start.30 = (bf16[64,384]{1,0:T(8,128)(2,1)S(1)}, bf16[64,384]{1,0:T(8,128)(2,1)S(1)}, u32[]{:S(2)}, u32[]{:S(2)}) collective-permute-start(bf16[64,384]{1,0:T(8,128)(2,1)S(1)} %get-tuple-element.114), channel_id=1, source_target_pairs={{0,2},{1,3},{2,4},{3,5},{4,6},{5,7},{6,0},{7,1},{8,10},{9,11},{10,... | collective-permute-start | bytes 147464 | tf_op jit(solution)/shard_map/ppermute | solution.py:502
  182.9 9.1 %collective-permute-start.31 = (bf16[64,384]{1,0:T(8,128)(2,1)S(1)}, bf16[64,384]{1,0:T(8,128)(2,1)S(1)}, u32[]{:S(2)}, u32[]{:S(2)}) collective-permute-start(bf16[64,384]{1,0:T(8,128)(2,1)S(1)} %get-tuple-element.116), channel_id=1, source_target_pairs={{0,4},{1,5},{2,6},{3,7},{4,0},{5,1},{6,2},{7,3},{8,12},{9,13},{10,... | collective-permute-start | bytes 147464 | tf_op jit(solution)/shard_map/ppermute | solution.py:502
  185.8 6.2 %collective-permute-start.32 = (bf16[64,384]{1,0:T(8,128)(2,1)S(1)}, bf16[64,384]{1,0:T(8,128)(2,1)S(1)}, u32[]{:S(2)}, u32[]{:S(2)}) collective-permute-start(bf16[64,384]{1,0:T(8,128)(2,1)S(1)} %get-tuple-element.115), channel_id=1, source_target_pairs={{0,6},{1,7},{2,0},{3,1},{4,2},{5,3},{6,4},{7,5},{8,14},{9,15},{10,... | collective-permute-start | bytes 147464 | tf_op jit(solution)/shard_map/ppermute | solution.py:502
  186.9 7.8 %collective-permute-start.38 = (bf16[64,1152]{1,0:T(8,128)(2,1)S(1)}, bf16[64,1152]{1,0:T(8,128)(2,1)S(1)}, u32[]{:S(2)}, u32[]{:S(2)}) collective-permute-start(bf16[64,1152]{1,0:T(8,128)(2,1)S(1)} %get-tuple-element.97), channel_id=1, source_target_pairs={{0,2},{1,3},{2,4},{3,5},{4,6},{5,7},{6,0},{7,1},{8,10},{9,11},{10,... | collective-permute-start | bytes 442376 | tf_op jit(solution)/shard_map/ppermute | solution.py:502
  187.9 11.4 %collective-permute-start.39 = (bf16[64,1152]{1,0:T(8,128)(2,1)S(1)}, bf16[64,1152]{1,0:T(8,128)(2,1)S(1)}, u32[]{:S(2)}, u32[]{:S(2)}) collective-permute-start(bf16[64,1152]{1,0:T(8,128)(2,1)S(1)} %get-tuple-element.99), channel_id=1, source_target_pairs={{0,4},{1,5},{2,6},{3,7},{4,0},{5,1},{6,2},{7,3},{8,12},{9,13},{10,... | collective-permute-start | bytes 442376 | tf_op jit(solution)/shard_map/ppermute | solution.py:502
  188.0 11.3 %collective-permute-start.40 = (bf16[64,1152]{1,0:T(8,128)(2,1)S(1)}, bf16[64,1152]{1,0:T(8,128)(2,1)S(1)}, u32[]{:S(2)}, u32[]{:S(2)}) collective-permute-start(bf16[64,1152]{1,0:T(8,128)(2,1)S(1)} %get-tuple-element.98), channel_id=1, source_target_pairs={{0,6},{1,7},{2,0},{3,1},{4,2},{5,3},{6,4},{7,5},{8,14},{9,15},{10,... | collective-permute-start | bytes 442376 | tf_op jit(solution)/shard_map/ppermute | solution.py:502
  192.1 8.8 %collective-permute-start.33 = (bf16[66,384]{1,0:T(8,128)(2,1)S(1)}, bf16[66,384]{1,0:T(8,128)(2,1)S(1)}, u32[]{:S(2)}, u32[]{:S(2)}) collective-permute-start(bf16[66,384]{1,0:T(8,128)(2,1)S(1)} %pad_maximum_fusion.11), channel_id=1, source_target_pairs={{0,24},{1,25},{2,26},{3,27},{4,28},{5,29},{6,30},{7,31},{8,16},{9,... | collective-permute-start | bytes 152072 | tf_op jit(solution)/shard_map/ppermute | solution.py:502
  192.1 9.2 %collective-permute-start.34 = (bf16[66,384]{1,0:T(8,128)(2,1)S(1)}, bf16[66,384]{1,0:T(8,128)(2,1)S(1)}, u32[]{:S(2)}, u32[]{:S(2)}) collective-permute-start(bf16[66,384]{1,0:T(8,128)(2,1)S(1)} %pad_maximum_fusion.11), channel_id=1, source_target_pairs={{0,16},{1,17},{2,18},{3,19},{4,20},{5,21},{6,22},{7,23},{8,24},{9,... | collective-permute-start | bytes 152072 | tf_op jit(solution)/shard_map/ppermute | solution.py:502
  194.7 6.6 %collective-permute-start.35 = (bf16[66,384]{1,0:T(8,128)(2,1)S(1)}, bf16[66,384]{1,0:T(8,128)(2,1)S(1)}, u32[]{:S(2)}, u32[]{:S(2)}) collective-permute-start(bf16[66,384]{1,0:T(8,128)(2,1)S(1)} %pad_maximum_fusion.11), channel_id=1, source_target_pairs={{0,8},{1,9},{2,10},{3,11},{4,12},{5,13},{6,14},{7,15},{8,0},{9,1},... | collective-permute-start | bytes 152072 | tf_op jit(solution)/shard_map/ppermute | solution.py:502
  199.4 6.2 %collective-permute-start.41 = (bf16[64,1152]{1,0:T(8,128)(2,1)S(1)}, bf16[64,1152]{1,0:T(8,128)(2,1)S(1)}, u32[]{:S(2)}, u32[]{:S(2)}) collective-permute-start(bf16[64,1152]{1,0:T(8,128)(2,1)S(1)} %add_convert_fusion.6), channel_id=1, source_target_pairs={{0,24},{1,25},{2,26},{3,27},{4,28},{5,29},{6,30},{7,31},{8,16},{9,... | collective-permute-start | bytes 442376 | tf_op jit(solution)/shard_map/ppermute | solution.py:502
  199.5 9.0 %collective-permute-start.42 = (bf16[64,1152]{1,0:T(8,128)(2,1)S(1)}, bf16[64,1152]{1,0:T(8,128)(2,1)S(1)}, u32[]{:S(2)}, u32[]{:S(2)}) collective-permute-start(bf16[64,1152]{1,0:T(8,128)(2,1)S(1)} %add_convert_fusion.6), channel_id=1, source_target_pairs={{0,16},{1,17},{2,18},{3,19},{4,20},{5,21},{6,22},{7,23},{8,24},{9,... | collective-permute-start | bytes 442376 | tf_op jit(solution)/shard_map/ppermute | solution.py:502
  200.8 7.6 %collective-permute-start.43 = (bf16[64,1152]{1,0:T(8,128)(2,1)S(1)}, bf16[64,1152]{1,0:T(8,128)(2,1)S(1)}, u32[]{:S(2)}, u32[]{:S(2)}) collective-permute-start(bf16[64,1152]{1,0:T(8,128)(2,1)S(1)} %add_convert_fusion.6), channel_id=1, source_target_pairs={{0,8},{1,9},{2,10},{3,11},{4,12},{5,13},{6,14},{7,15},{8,0},{9,1},... | collective-permute-start | bytes 442376 | tf_op jit(solution)/shard_map/ppermute | solution.py:502
  208.8 2.4 %copy-start.1 = (bf16[64,1536]{1,0:T(8,128)(2,1)S(1)}, bf16[64,1536]{1,0:T(8,128)(2,1)}, u32[]{:S(2)}) copy-start(bf16[64,1536]{1,0:T(8,128)(2,1)} %param.16) | copy-start | bytes 589828
